TPU v7x, 32 devices: a whole 2x2x4 slice. The times are simulated.
32 devices in a mesh: fsdp: 32 (over z, y, x, core).
Axes of the slice: x: 2, y: 2, z: 4, core: 2. Of those that a mesh axis runs over, the one named last changes fastest.
Arguments:
- tokens: bfloat16 [4096, 768], P('fsdp'), may hold values from -6 to 6
- seq_lengths: int32 [32, 8], P('fsdp'), may hold values from 1 to 64, 128 in all within a row
- cotangent: bfloat16 [4096, 768], P('fsdp'), may hold values from -6 to 6
- wide_weights: float32 [768, 6144], P('fsdp'), may hold values from -2 to 2
- proj_weights: float32 [3072, 768], P('fsdp'), may hold values from -0.109375 to 0.109375
- vector_params: float32 [12, 768], P(None, 'fsdp'), may hold values from -1 to 1.5
- wide_moments: float32 [2, 768, 6144], P(None, 'fsdp'), may hold values from -0.16 to 0.16, as said below
- proj_moments: float32 [2, 3072, 768], P(None, 'fsdp'), may hold values from -0.16 to 0.16, as said below
- vector_moments: float32 [2, 12, 768], P(None, None, 'fsdp'), may hold values from -0.16 to 0.16, as said below
Outputs:
- block_output: bfloat16 [4096, 768], P('fsdp')
- tokens_grad: bfloat16 [4096, 768], P('fsdp')
- wide_grad: float32 [768, 6144], P('fsdp')
- proj_grad: float32 [3072, 768], P('fsdp')
- vector_grad: float32 [12, 768], P(None, 'fsdp')
- wide_new: float32 [768, 6144], P('fsdp')
- proj_new: float32 [3072, 768], P('fsdp')
- vector_new: float32 [12, 768], P(None, 'fsdp')
- wide_moments_new: float32 [2, 768, 6144], P(None, 'fsdp')
- proj_moments_new: float32 [2, 3072, 768], P(None, 'fsdp')
- vector_moments_new: float32 [2, 12, 768], P(None, None, 'fsdp')
Inputs may be any that keep to these rules, and one draw needn't show every extreme that they name: `seq_lengths`: row s holds the lengths of the 8 sequences of device slice s; every row sums to 128 and its largest entry is 64. `wide_moments`: index 0 of the leading dimension holds first moments, index 1 second moments, which are positive. `proj_moments`: index 0 of the leading dimension holds first moments, index 1 second moments, which are positive. `vector_moments`: index 0 of the leading dimension holds first moments, index 1 second moments, which are positive.
All inputs are finite; a program needn't handle non-finite values.
Results may differ from a plain program's by a relative error of at most 0.012.
The roundings to bfloat16 on the way count: a program that leaves them out, or rounds other values in their place, can miss the bound.
Values may be sent and summed in bfloat16 or wider, within the bound.
A program may use at most 192 MiB of HBM per device.

v0:
```python
import math

import jax
import jax.numpy as jnp
from jax import lax
from jax.sharding import PartitionSpec as P

D = 768
H = 12
HD = 64
FF = 3072
STEP = 2


norm_eps = 1e-05
beta_one = 0.9
beta_two = 0.95
adam_eps = 1e-08
rate_matrix = 0.02
rate_vector = 0.2
weight_decay = 0.1
gelu_coeff = 0.7978845608028654
masked_score = -1e30


def norm_forward(values, gain_row, offset):
    center = values - jnp.mean(values, axis=1, keepdims=True)
    variance = jnp.mean(center * center, axis=1, keepdims=True)
    inverse = lax.rsqrt(variance + norm_eps)
    normed = center * inverse
    return (normed * gain_row + offset, normed, inverse)


def norm_backward(upstream, normed, inverse, gain_row):
    scaled = upstream * gain_row
    mean_term = jnp.mean(scaled, axis=1, keepdims=True)
    proj_term = jnp.mean(scaled * normed, axis=1, keepdims=True)
    input_grad = inverse * (scaled - mean_term - normed * proj_term)
    return (input_grad, jnp.sum(upstream * normed, axis=0), jnp.sum(upstream, axis=0))


def gelu_parts(before):
    inner_arg = gelu_coeff * (before + 0.044715 * before * before * before)
    tangent = jnp.tanh(inner_arg)
    value_part = 0.5 * before * (1.0 + tangent)
    slope_part = 0.5 * (1.0 + tangent) + 0.5 * before * (1.0 - tangent * tangent) * gelu_coeff * (
        1.0 + 3.0 * 0.044715 * before * before
    )
    return (value_part, slope_part)


def allowed_pairs(length_row, row_count):
    bounds = jnp.cumsum(length_row)
    position = jnp.arange(row_count, dtype=jnp.int32)
    segment = jnp.sum((position[:, None] >= bounds[None, :]).astype(jnp.int32), axis=1)
    return (segment[:, None] == segment[None, :]) & (position[None, :] <= position[:, None])


def head_view(matrix):
    return matrix.reshape(matrix.shape[0], H, HD)


def score_table(queries, key_rows, allowed):
    scale_factor = 1.0 / math.sqrt(HD)
    scores = (
        jnp.einsum(
            "qhd,khd->hqk",
            head_view(queries),
            head_view(key_rows),
            preferred_element_type=jnp.float32,
        )
        * scale_factor
    )
    return jnp.where(allowed[None, :, :], scores, masked_score)


def attention_forward(queries, key_rows, value_rows, allowed):
    scores = score_table(queries, key_rows, allowed)
    highest = jnp.max(scores, axis=2, keepdims=True)
    logsum = highest + jnp.log(jnp.sum(jnp.exp(scores - highest), axis=2, keepdims=True))
    weights = jnp.exp(scores - logsum).astype(jnp.bfloat16)
    mixed = jnp.einsum(
        "hqk,khd->qhd", weights, head_view(value_rows), preferred_element_type=jnp.float32
    )
    return (mixed.reshape(queries.shape[0], D).astype(jnp.bfloat16), logsum)


def attention_backward(queries, key_rows, value_rows, allowed, logsum, upstream):
    scale_factor = 1.0 / math.sqrt(HD)
    scores = score_table(queries, key_rows, allowed)
    probs = jnp.exp(scores - logsum)
    rounded = probs.astype(jnp.bfloat16)
    grad_heads = head_view(upstream)
    value_grad = jnp.einsum("hqk,qhd->khd", rounded, grad_heads, preferred_element_type=jnp.float32)
    prob_grad = jnp.einsum(
        "qhd,khd->hqk", grad_heads, head_view(value_rows), preferred_element_type=jnp.float32
    )
    delta_row = jnp.sum(probs * prob_grad, axis=2, keepdims=True)
    score_grad = (probs * (prob_grad - delta_row) * scale_factor).astype(jnp.bfloat16)
    query_grad = jnp.einsum(
        "hqk,khd->qhd", score_grad, head_view(key_rows), preferred_element_type=jnp.float32
    )
    key_grad = jnp.einsum(
        "hqk,qhd->khd", score_grad, head_view(queries), preferred_element_type=jnp.float32
    )
    row_total = queries.shape[0]
    joined = jnp.concatenate(
        [
            query_grad.reshape(row_total, D),
            key_grad.reshape(row_total, D),
            value_grad.reshape(row_total, D),
        ],
        axis=1,
    )
    return joined.astype(jnp.bfloat16)


def adam_update(weights, moments, gradient, rate, decay_rate, unscale):
    scaled_grad = gradient / unscale
    first_moment = beta_one * moments[0] + (1.0 - beta_one) * scaled_grad
    second_moment = beta_two * moments[1] + (1.0 - beta_two) * scaled_grad * scaled_grad
    corrected_first = first_moment / (1.0 - beta_one**STEP)
    corrected_second = second_moment / (1.0 - beta_two**STEP)
    updated = weights - rate * (
        corrected_first / (jnp.sqrt(corrected_second) + adam_eps) + decay_rate * weights
    )
    return (updated, jnp.stack([first_moment, second_moment]))


def column_term(left, right):
    return jnp.einsum("tc,te->ce", left, right, preferred_element_type=jnp.float32)


def body(
    tokens,
    seq_lengths,
    cotangent,
    wide_weights,
    proj_weights,
    vector_params,
    wide_moments,
    proj_moments,
    vector_moments,
):
    shards = (
        wide_weights.astype(jnp.bfloat16),
        proj_weights.astype(jnp.bfloat16),
        vector_params.astype(jnp.bfloat16),
    )
    wide_full, proj_full, vector_full = (
        lax.all_gather(shards[0], "fsdp", axis=0, tiled=True),
        lax.all_gather(shards[1], "fsdp", axis=0, tiled=True),
        lax.all_gather(shards[2], "fsdp", axis=1, tiled=True),
    )
    vectors = vector_full.astype(jnp.float32)
    row_count = tokens.shape[0]
    allowed = allowed_pairs(seq_lengths[0], row_count)
    ratio = FF // D
    local_rows = wide_weights.shape[0]
    unscale = math.sqrt(lax.axis_size("fsdp") * row_count)
    gain_one, shift_one, query_bias, value_bias = (vectors[0], vectors[1], vectors[2], vectors[3])
    out_bias, gain_two, shift_two, proj_bias = (vectors[4], vectors[5], vectors[6], vectors[7])
    fc_bias = vectors[8:].reshape(FF)
    token_float = tokens.astype(jnp.float32)
    first_norm, normed_one, inverse_one = norm_forward(token_float, gain_one, shift_one)
    first_in = first_norm.astype(jnp.bfloat16)
    qkv_bias = jnp.concatenate([query_bias, jnp.zeros_like(query_bias), value_bias])
    qkv_half = (
        jnp.dot(first_in, wide_full[:, : 3 * D], preferred_element_type=jnp.float32) + qkv_bias
    ).astype(jnp.bfloat16)
    queries = qkv_half[:, :D]
    key_rows = qkv_half[:, D : 2 * D]
    value_rows = qkv_half[:, 2 * D :]
    attended, logsum = attention_forward(queries, key_rows, value_rows, allowed)
    residual = (
        token_float
        + jnp.dot(attended, wide_full[:, 3 * D : 4 * D], preferred_element_type=jnp.float32)
        + out_bias
    )
    second_norm, normed_two, inverse_two = norm_forward(residual, gain_two, shift_two)
    second_in = second_norm.astype(jnp.bfloat16)
    before_act = (
        jnp.dot(second_in, wide_full[:, 4 * D :], preferred_element_type=jnp.float32) + fc_bias
    )
    value_part, slope_part = gelu_parts(before_act)
    hidden = value_part.astype(jnp.bfloat16)
    block_output = (
        residual + jnp.dot(hidden, proj_full, preferred_element_type=jnp.float32) + proj_bias
    ).astype(jnp.bfloat16)
    backward_wide, backward_proj, vector_again = (
        lax.all_gather(shards[0], "fsdp", axis=0, tiled=True),
        lax.all_gather(shards[1], "fsdp", axis=0, tiled=True),
        lax.all_gather(shards[2], "fsdp", axis=1, tiled=True),
    )
    backward_vectors = vector_again.astype(jnp.float32)
    qkv_back = backward_wide[:, : 3 * D]
    out_back = backward_wide[:, 3 * D : 4 * D]
    fc_back = backward_wide[:, 4 * D :]
    cot_float = cotangent.astype(jnp.float32)
    proj_bias_grad = jnp.sum(cot_float, axis=0)
    hidden_grad = jnp.einsum(
        "td,fd->tf", cotangent, backward_proj, preferred_element_type=jnp.float32
    )
    pre_grad = (hidden_grad * slope_part).astype(jnp.bfloat16)
    fc_bias_grad = jnp.sum(pre_grad, axis=0, dtype=jnp.float32)
    second_grad = jnp.einsum("tf,df->td", pre_grad, fc_back, preferred_element_type=jnp.float32)
    resid_norm_grad, gain_two_grad, shift_two_grad = norm_backward(
        second_grad, normed_two, inverse_two, backward_vectors[5]
    )
    resid_grad = cot_float + resid_norm_grad
    mlp_vectors = jnp.concatenate(
        [
            jnp.stack([gain_two_grad, shift_two_grad, proj_bias_grad]),
            fc_bias_grad.reshape(ratio, D),
        ],
        axis=0,
    )
    resid_half = resid_grad.astype(jnp.bfloat16)
    out_bias_grad = jnp.sum(resid_grad, axis=0)
    attended_grad = jnp.einsum(
        "te,de->td", resid_half, out_back, preferred_element_type=jnp.float32
    ).astype(jnp.bfloat16)
    qkv_grad = attention_backward(queries, key_rows, value_rows, allowed, logsum, attended_grad)
    query_bias_grad = jnp.sum(qkv_grad[:, :D], axis=0, dtype=jnp.float32)
    value_bias_grad = jnp.sum(qkv_grad[:, 2 * D :], axis=0, dtype=jnp.float32)
    first_grad = jnp.einsum("tc,dc->td", qkv_grad, qkv_back, preferred_element_type=jnp.float32)
    token_norm_grad, gain_one_grad, shift_one_grad = norm_backward(
        first_grad, normed_one, inverse_one, backward_vectors[0]
    )
    tokens_grad = (resid_grad + token_norm_grad).astype(jnp.bfloat16)
    attn_vectors = jnp.stack(
        [gain_one_grad, shift_one_grad, query_bias_grad, value_bias_grad, out_bias_grad]
    )
    fc_part = column_term(second_in, pre_grad)
    proj_part = column_term(hidden, cotangent).reshape(
        local_rows * lax.axis_size("fsdp"), ratio * D
    )
    qkv_part = column_term(first_in, qkv_grad)
    out_part = column_term(attended, resid_half)
    joined_shard = lax.psum_scatter(
        jnp.concatenate(
            [
                jnp.concatenate([qkv_part, out_part], axis=1),
                jnp.concatenate([fc_part, proj_part], axis=1),
            ],
            axis=1,
        ),
        "fsdp",
        scatter_dimension=0,
        tiled=True,
    )
    wide_grad = joined_shard[:, : 4 * D + FF]
    proj_grad = joined_shard[:, 4 * D + FF :].reshape(local_rows * ratio, D)
    vector_terms = jnp.concatenate([attn_vectors, mlp_vectors], axis=0)
    vector_grad = lax.psum_scatter(vector_terms, "fsdp", scatter_dimension=1, tiled=True)
    wide_new, wide_moments_new = adam_update(
        wide_weights, wide_moments, wide_grad, rate_matrix, weight_decay, unscale
    )
    proj_new, proj_moments_new = adam_update(
        proj_weights, proj_moments, proj_grad, rate_matrix, weight_decay, unscale
    )
    vector_new, vector_moments_new = adam_update(
        vector_params, vector_moments, vector_grad, rate_vector, 0.0, unscale
    )
    return (
        block_output,
        tokens_grad,
        wide_grad,
        proj_grad,
        vector_grad,
        wide_new,
        proj_new,
        vector_new,
        wide_moments_new,
        proj_moments_new,
        vector_moments_new,
    )


def solution(mesh):
    placed = (
        P("fsdp", None),
        P("fsdp", None),
        P("fsdp", None),
        P("fsdp", None),
        P("fsdp", None),
        P(None, "fsdp"),
        P(None, "fsdp", None),
        P(None, "fsdp", None),
        P(None, None, "fsdp"),
    )
    return jax.shard_map(
        body,
        mesh=mesh,
        in_specs=placed,
        out_specs=(
            P("fsdp", None),
            P("fsdp", None),
            P("fsdp", None),
            P("fsdp", None),
            P(None, "fsdp"),
            P("fsdp", None),
            P("fsdp", None),
            P(None, "fsdp"),
            P(None, "fsdp", None),
            P(None, "fsdp", None),
            P(None, None, "fsdp"),
        ),
        check_vma=False,
    )
```

profile of v0, /device:TPU:0, one launch (start us, length us, event | category | flops | bytes accessed | tf_op | source)
XLA Modules:
  0.0 502.7 jit_solution(7612656013296215332)
XLA Ops:
  7.3 1.9 convert_element_type.79
  9.2 1.6 convert_element_type.88
  10.9 44.3 %all-gather = bf16[32,24,12]{1,2,0:T(8,128)(2,1)S(1)} all-gather(bf16[1,24,12]{1,2,0:T(8,128)(2,1)S(1)} %convert_bitcast_fusion), channel_id=1, replica_groups=mesh['fsdp'=32] {'fsdp'}, dimensions={0}, use_global_device_ids=true | all-gather | bytes 19008 | tf_op jit(solution)/shard_map/all_gather | solution.py:153
  57.6 38.9 %all-gather.4.cloned.1.call-done = bf16[768,6144]{1,0:T(8,128)(2,1)} async-done(((bf16[24,6144]{1,0:T(8,128)(2,1)}), bf16[768,6144]{1,0:T(8,128)(2,1)}) %all-gather.4.cloned.1.call-update) | async-done | bytes 9437200 | tf_op jit(solution)/shard_map/all_gather | solution.py:151
  96.4 2.7 fusion.9
  100.5 1.8 fusion.93
  103.1 3.2 fusion.5
  106.4 55.9 %all-gather.6.cloned.1.call-done = bf16[3072,768]{1,0:T(8,128)(2,1)} async-done(((bf16[96,768]{1,0:T(8,128)(2,1)}), bf16[3072,768]{1,0:T(8,128)(2,1)}) %all-gather.6.cloned.1.call-update) | async-done | bytes 4718608 | tf_op jit(solution)/shard_map/all_gather | solution.py:152
  162.2 4.8 convert_reduce_fusion
  167.0 5.0 %multiply_reduce_fusion.1 = (f32[768]{0:T(1024)}, f32[128]{0:T(128)S(1)}, f32[128]{0:T(128)S(1)}, f32[768]{0:T(1024)}, f32[128,768]{1,0:T(8,128)S(1)}) fusion(f32[128,768]{1,0:T(8,128)S(1)} %get-tuple-element.95, f32[128]{0:T(128)S(1)} %copy-done.43, f32[128]{0:T(128)S(1)} %copy-done.37, f32[768]{0:T(1024)S(1)} %get-tuple-element.63, ...), kind=kOutput, calls=%fused_computation.72 | convolution fusion | flops 604862720 | bytes 6302720 | tf_op jit(solution)/shard_map/tf,df->td/dot_general | solution.py:206
  172.9 1.8 convolution_convert_fusion.3
  174.9 1.1 convolution_convert_fusion
  176.3 1.1 convolution_convert_fusion.2
  177.4 1.1 convolution_convert_fusion.1
  178.9 1.0 copy-done.2
  179.9 5.2 %fusion.88 = f32[3072,768]{1,0:T(8,128)} fusion(bf16[128,768]{1,0:T(8,128)(2,1)S(1)} %copy-done.15, f32[128,3072]{1,0:T(8,128)S(1)} %copy-done.2), kind=kOutput, calls=%fused_computation.148 | convolution fusion | flops 607518720 | bytes 11206656 | tf_op jit(solution)/shard_map/tc,te->ce/dot_general | solution.py:131
  185.1 5.0 %fusion.87 = f32[768,3072]{1,0:T(8,128)} fusion(bf16[128,3072]{1,0:T(8,128)(2,1)S(1)} %copy-done.17, f32[128,768]{1,0:T(8,128)S(1)} %get-tuple-element.95, f32[768]{0:T(1024)S(1)} %get-tuple-element.65, f32[768]{0:T(1024)S(1)} %get-tuple-element.63, f32[128]{0:T(128)S(1)} %copy-done.44, f32[128]{0:T(128)S(1)} %copy-done.38), kind=kOutput, calls=%fused_computation.147 | convolution fusion | flops 604471296 | bytes 10624000 | tf_op jit(solution)/shard_map/tc,te->ce/dot_general | solution.py:131
  190.1 11.6 %reshape.238 = f32[768,3072]{1,0:T(8,128)} reshape(f32[3072,768]{1,0:T(8,128)} %fusion.88) | data formatting | bytes 18874368 | tf_op jit(solution)/shard_map/reshape | solution.py:235
  201.7 5.1 %fusion.64 = f32[768,2304]{1,0:T(8,128)} fusion(bf16[128,768]{0,1:T(8,128)(2,1)S(1)} %bitcast.109, bf16[128,768]{0,1:T(8,128)(2,1)} %bitcast.117, bf16[128,768]{0,1:T(8,128)(2,1)} %bitcast.115, bf16[128,768]{1,0:T(8,128)(2,1)S(1)} %copy-done, f32[768]{0:T(1024)S(1)} %get-tuple-element.69, f32[768]{0:T(1024)S(1)} %get-tuple-element.70, ...), kind=kOutput, calls=%fused_computation.100 | convolution fusion | flops 455344128 | bytes 7871488 | tf_op jit(solution)/shard_map/tc,te->ce/dot_general | solution.py:131
  206.8 19.5 %pad_maximum_fusion = f32[768,9216]{1,0:T(8,128)} fusion(f32[768,3072]{1,0:T(8,128)} %reshape.238, f32[768,3072]{1,0:T(8,128)} %fusion.87, f32[768,768]{1,0:T(8,128)S(1)} %fusion.68, f32[768,2304]{1,0:T(8,128)} %fusion.64), kind=kLoop, calls=%fused_computation.1 | loop fusion | flops 21233664 | bytes 56623104 | tf_op jit(solution)/shard_map/concatenate | solution.py:241
  230.8 4.0 fusion.46
  234.9 1.7 concatenate.16
  236.7 40.4 %all-reduce = f32[12,768]{1,0:T(8,128)S(1)} all-reduce(f32[12,768]{1,0:T(8,128)S(1)} %concatenate.16), channel_id=3, replica_groups=mesh['fsdp'=32] {'fsdp'}, use_global_device_ids=true, to_apply=%region_23.24.clone | all-reduce | flops 9216 | bytes 73728
  277.2 1.4 fusion.78
  280.5 1.5 fusion.45
  282.0 4.1 fusion.25
  286.1 203.1 %reduce-scatter.3.cloned.1.call-done = f32[24,9216]{1,0:T(8,128)} async-done(((f32[768,9216]{1,0:T(8,128)}), f32[24,9216]{1,0:T(8,128)}) %reduce-scatter.3.cloned.1.call-update) | async-done | bytes 884752 | tf_op jit(solution)/shard_map/reduce_scatter | solution.py:240
  489.1 1.0 broadcast_multiply_fusion
  490.5 1.3 fusion.65
  491.8 1.3 fusion.71
  493.2 1.0 fusion.60
  495.1 1.1 pad_maximum_fusion.1
  (157 shorter events, 14.1 us)
Async XLA Ops:
  7.2 3.7 copy-start.26
  7.2 49.0 %copy-start.48 = (s32[1,8]{1,0:T(1,128)S(1)}, s32[1,8]{1,0:T(1,128)}, u32[]{:S(2)}) copy-start(s32[1,8]{1,0:T(1,128)} %param.10) | copy-start | bytes 100
  7.2 49.9 %copy-start = (bf16[128,768]{1,0:T(8,128)(2,1)S(1)}, bf16[128,768]{1,0:T(8,128)(2,1)}, u32[]{:S(2)}) copy-start(bf16[128,768]{1,0:T(8,128)(2,1)} %param.9) | copy-start | bytes 589828
  7.2 89.2 %all-gather.4.cloned.1.call-start = ((), (), s32[]{:S(2)}) async-start(), calls=%async_computation.1 | async-start | bytes 9732096 | tf_op jit(solution)/shard_map/all_gather | solution.py:151
  9.1 153.1 %all-gather.6.cloned.1.call-start = ((), (), s32[]{:S(2)}) async-start(), calls=%async_computation.2 | async-start | bytes 4866048 | tf_op jit(solution)/shard_map/all_gather | solution.py:152
  10.9 478.3 %reduce-scatter.3.cloned.1.call-start = ((), (), s32[]{:S(2)}) async-start(), calls=%async_computation.3 | async-start | bytes 29196288 | tf_op jit(solution)/shard_map/reduce_scatter | solution.py:240
  57.2 41.9 %copy-start.33 = (f32[128]{0:T(128)}, f32[128]{0:T(128)S(1)}, u32[]{:S(2)}) copy-start(f32[128]{0:T(128)S(1)} %broadcast_multiply_fusion.6) | copy-start | bytes 1540
  57.5 41.7 %copy-start.39 = (f32[128]{0:T(128)}, f32[128]{0:T(128)S(1)}, u32[]{:S(2)}) copy-start(f32[128]{0:T(128)S(1)} %add_rsqrt_fusion.1) | copy-start | bytes 1540
  100.2 2.9 copy-start.32
  100.5 5.9 %copy-start.8 = (bf16[12,64,128]{2,1,0:T(8,128)(2,1)}, bf16[12,64,128]{2,1,0:T(8,128)(2,1)S(1)}, u32[]{:S(2)}) copy-start(bf16[12,64,128]{2,1,0:T(8,128)(2,1)S(1)} %convolution_convert_fusion.4) | copy-start | bytes 589828
  103.1 59.1 %copy-start.13 = (bf16[128,768]{1,0:T(8,128)(2,1)S(1)}, bf16[128,768]{1,0:T(8,128)(2,1)}, u32[]{:S(2)}) copy-start(bf16[128,768]{1,0:T(8,128)(2,1)} %param.11) | copy-start | bytes 589828
  106.3 60.7 %copy-start.1 = (f32[128,3072]{1,0:T(8,128)}, f32[128,3072]{1,0:T(8,128)S(1)}, u32[]{:S(2)}) copy-start(f32[128,3072]{1,0:T(8,128)S(1)} %fusion.5) | copy-start | bytes 4718596
  162.2 4.8 copy-start.37
  162.2 4.8 copy-start.43
  167.0 5.1 %copy-start.16 = (bf16[128,3072]{1,0:T(8,128)(2,1)}, bf16[128,3072]{1,0:T(8,128)(2,1)S(1)}, u32[]{:S(2)}) copy-start(bf16[128,3072]{1,0:T(8,128)(2,1)S(1)} %get-tuple-element.99) | copy-start | bytes 2359300
  167.0 5.1 %copy-start.14 = (bf16[128,768]{1,0:T(8,128)(2,1)S(1)}, bf16[128,768]{1,0:T(8,128)(2,1)}, u32[]{:S(2)}) copy-start(bf16[128,768]{1,0:T(8,128)(2,1)} %param.11) | copy-start | bytes 589828
  172.1 2.8 copy-start.25
  179.9 5.2 %copy-start.17 = (bf16[128,3072]{1,0:T(8,128)(2,1)S(1)}, bf16[128,3072]{1,0:T(8,128)(2,1)}, u32[]{:S(2)}) copy-start(bf16[128,3072]{1,0:T(8,128)(2,1)} %copy-done.16) | copy-start | bytes 2359300
  179.9 5.2 %copy-start.38 = (f32[128]{0:T(128)S(1)}, f32[128]{0:T(128)}, u32[]{:S(2)}) copy-start(f32[128]{0:T(128)} %copy-done.36) | copy-start | bytes 1540
  179.9 5.2 %copy-start.44 = (f32[128]{0:T(128)S(1)}, f32[128]{0:T(128)}, u32[]{:S(2)}) copy-start(f32[128]{0:T(128)} %copy-done.42) | copy-start | bytes 1540
  190.1 11.6 %copy-start.10 = (bf16[12,64,128]{2,1,0:T(8,128)(2,1)S(1)}, bf16[12,64,128]{2,1,0:T(8,128)(2,1)}, u32[]{:S(2)}) copy-start(bf16[12,64,128]{2,1,0:T(8,128)(2,1)} %convolution_convert_fusion) | copy-start | bytes 589828
  190.1 11.6 %copy-start.34 = (f32[128]{0:T(128)S(1)}, f32[128]{0:T(128)}, u32[]{:S(2)}) copy-start(f32[128]{0:T(128)} %copy-done.33) | copy-start | bytes 1540
  190.1 11.6 %copy-start.40 = (f32[128]{0:T(128)S(1)}, f32[128]{0:T(128)}, u32[]{:S(2)}) copy-start(f32[128]{0:T(128)} %copy-done.39) | copy-start | bytes 1540
  226.4 3.1 copy-start.28
  226.4 4.4 copy-start.22
  226.4 4.4 copy-start.23
  226.4 4.3 copy-start.35
  226.4 4.3 copy-start.41
  234.8 47.2 %copy-start.3 = (f32[128,3072]{1,0:T(8,128)S(1)}, f32[128,3072]{1,0:T(8,128)}, u32[]{:S(2)}) copy-start(f32[128,3072]{1,0:T(8,128)} %copy-done.1) | copy-start | bytes 4718596
  234.8 47.2 %copy-start.45 = (f32[768]{0:T(1024)S(1)}, f32[768]{0:T(1024)}, u32[]{:S(2)}) copy-start(f32[768]{0:T(1024)} %get-tuple-element.64) | copy-start | bytes 9220
  277.2 8.9 %copy-start.27 = (f32[12,24]{1,0:T(8,128)}, f32[12,24]{1,0:T(8,128)S(1)}, u32[]{:S(2)}) copy-start(f32[12,24]{1,0:T(8,128)S(1)} %get-tuple-element.72) | copy-start | bytes 3460
  286.1 204.4 %copy-start.4 = (f32[2,24,6144]{2,1,0:T(8,128)S(1)}, f32[2,24,6144]{2,1,0:T(8,128)}, u32[]{:S(2)}) copy-start(f32[2,24,6144]{2,1,0:T(8,128)} %param.15) | copy-start | bytes 3538948
  (20 other events, 29.9 us)
Sparse Core Ops, SparseCore 0:
  11.5 84.8 all-gather.3
  99.9 62.2 all-gather.5
  226.6 262.4 reduce-scatter.2
where the time goes:
time: 504 us; the launch traced here: 503 us
  waiting for transfers between devices  298 us (59%)
  blocking collectives  84.7 us (17%)
  matrix products  47.3 us (9%)
  other arithmetic  36 us (7%)
  local copies, waits for them, and re-layouts  22.4 us (4%)
  between operations  14.3 us (3%)
    reduce_scatter x1, waiting for transfers between devices, body(): lax.psum_scatter(jnp.concatenate([jnp.concatenate([qkv_part, out_part], a...  203 us
    all_gather x1, waiting for transfers between devices, body(): lax.all_gather(shards[1], 'fsdp', axis=0, tiled=True)  55.9 us
    all_gather x1, blocking collectives, body(): lax.all_gather(shards[2], 'fsdp', axis=1, tiled=True)  44.3 us
    unnamed x1, blocking collectives  40.4 us
    all_gather x1, waiting for transfers between devices, body(): lax.all_gather(shards[0], 'fsdp', axis=0, tiled=True)  38.9 us
    concatenate x1, other arithmetic, body(): jnp.concatenate([jnp.concatenate([qkv_part, out_part], axis=1), jnp.conca...  19.5 us
    dot_general x4, matrix products, column_term(): jnp.einsum('tc,te->ce', left, right, preferred_element_type=jnp.float32)  15.8 us
    reshape x1, local copies, waits for them, and re-layouts, body(): column_term(hidden, cotangent)  11.6 us
  transfers between devices with their start and end apart: 3, of which 3 were waited for; matrix products, arithmetic and copies ran while one was open for 6% of the time, Pallas kernels for 0%

commit v1 on v0

--- a/solution.py
+++ b/solution.py
@@ -1,8 +1,11 @@
+import functools
 import math
 
 import jax
 import jax.numpy as jnp
 from jax import lax
+from jax.experimental import pallas as pl
+from jax.experimental.pallas import tpu as pltpu
 from jax.sharding import PartitionSpec as P
 
 D = 768
@@ -129,6 +132,407 @@
 
 def column_term(left, right):
     return jnp.einsum("tc,te->ce", left, right, preferred_element_type=jnp.float32)
+
+
+MESH = pl.DeviceIdType.MESH
+WIDE_A = 6 * D
+GROUP = 24
+
+
+def position(n):
+    depth = n // 8
+    me = lax.axis_index("fsdp")
+    return depth, me // 8, (me // 4) % 2, (me // 2) % 2, me % 2
+
+
+def device_at(z, y, x, c):
+    return ((z * 2 + y) * 2 + x) * 2 + c
+
+
+def greet(partners):
+    barrier = pltpu.get_barrier_semaphore()
+    for device in partners:
+        pl.semaphore_signal(barrier, inc=1, device_id=(device,), device_id_type=MESH)
+    pl.semaphore_wait(barrier, len(partners))
+
+
+def remote(src, dst, send, recv, device):
+    return pltpu.make_async_remote_copy(
+        src_ref=src,
+        dst_ref=dst,
+        send_sem=send,
+        recv_sem=recv,
+        device_id=(device,),
+        device_id_type=MESH,
+    )
+
+
+def gather_kernel(n, wide, proj, vec, wide_out, proj_out, vec_out, local, ssem, rsem):
+    depth, z, y, x, c = position(n)
+    z_peers = [device_at((z + d) % depth, y, x, c) for d in range(1, depth)]
+    y_peer, x_peer = device_at(z, 1 - y, x, c), device_at(z, y, 1 - x, c)
+    core_peer = device_at(z, y, x, 1 - c)
+    greet(z_peers + [y_peer, x_peer, core_peer])
+    sends = []
+    count = [0]
+
+    def push(src, dst, device, landed):
+        k = count[0]
+        count[0] = k + 1
+        copy = remote(src, dst, ssem.at[k], rsem.at[k], device)
+        copy.start()
+        sends.append(copy)
+        return remote(landed, landed, ssem.at[k], rsem.at[k], device)
+
+    own = [
+        pltpu.make_async_copy(wide, wide_out.at[z, y, x, c], local.at[0]),
+        pltpu.make_async_copy(proj, proj_out.at[z, y, x, c], local.at[1]),
+        pltpu.make_async_copy(vec, vec_out.at[z, y, x, c], local.at[2]),
+    ]
+    for copy in own:
+        copy.start()
+
+    def wide_low(zi, p, q, ci):
+        return wide_out.at[zi, p, q, ci, :, pl.ds(0, WIDE_A)]
+
+    def wide_high(zi, p, q, ci):
+        return wide_out.at[zi, q, p, ci, :, pl.ds(WIDE_A, wide.shape[1] - WIDE_A)]
+
+    def proj_at(zi, p, q, ci):
+        return proj_out.at[zi, q, p, ci]
+
+    def vec_at(zi, p, q, ci):
+        return vec_out.at[zi, q, p, ci]
+
+    yx = (y, x, y_peer, x_peer)
+    xy = (x, y, x_peer, y_peer)
+    streams = [
+        (wide.at[:, pl.ds(0, WIDE_A)], wide_low, yx),
+        (wide.at[:, pl.ds(WIDE_A, wide.shape[1] - WIDE_A)], wide_high, xy),
+        (proj, proj_at, xy),
+        (vec, vec_at, xy),
+    ]
+    every = pl.ds(0, depth)
+    from_z = [[] for _ in streams]
+    from_first = [[] for _ in streams]
+    from_second = [[] for _ in streams]
+    from_far = [[] for _ in streams]
+    from_core = []
+    for d in range(1, depth):
+        for s, (mine, at, (p, q, _, _)) in enumerate(streams):
+            from_z[s].append(
+                push(mine, at(z, p, q, c), z_peers[d - 1], at((z + depth - d) % depth, p, q, c))
+            )
+    for s, (mine, at, (p, q, first, second)) in enumerate(streams):
+        from_first[s].append(push(mine, at(z, p, q, c), first, at(z, 1 - p, q, c)))
+        from_second[s].append(push(mine, at(z, p, q, c), second, at(z, p, 1 - q, c)))
+    for copy in own:
+        copy.wait()
+    for d in range(1, depth):
+        zi = (z + depth - d) % depth
+        for s, (mine, at, (p, q, first, second)) in enumerate(streams):
+            from_z[s][d - 1].wait_recv()
+            here = at(zi, p, q, c)
+            from_first[s].append(push(here, here, first, at(zi, 1 - p, q, c)))
+            from_second[s].append(push(here, here, second, at(zi, p, 1 - q, c)))
+    for mine, at, (p, q, _, _) in streams:
+        here = at(every, p, q, c)
+        from_core.append(push(here, here, core_peer, at(every, p, q, 1 - c)))
+    for d in range(depth):
+        zi = (z + depth - d) % depth
+        for s, (mine, at, (p, q, first, second)) in enumerate(streams):
+            from_first[s][d].wait_recv()
+            here = at(zi, 1 - p, q, c)
+            from_far[s].append(push(here, here, second, at(zi, 1 - p, 1 - q, c)))
+    for mine, at, (p, q, _, _) in streams:
+        here = at(every, 1 - p, q, c)
+        from_core.append(push(here, here, core_peer, at(every, 1 - p, q, 1 - c)))
+    for s, (mine, at, (p, q, _, _)) in enumerate(streams):
+        for d in range(depth):
+            from_second[s][d].wait_recv()
+        here = at(every, p, 1 - q, c)
+        from_core.append(push(here, here, core_peer, at(every, p, 1 - q, 1 - c)))
+    for s, (mine, at, (p, q, _, _)) in enumerate(streams):
+        for d in range(depth):
+            from_far[s][d].wait_recv()
+        here = at(every, 1 - p, 1 - q, c)
+        from_core.append(push(here, here, core_peer, at(every, 1 - p, 1 - q, 1 - c)))
+    for copy in from_core:
+        copy.wait_recv()
+    for copy in sends:
+        copy.wait_send()
+
+
+def gather_all(n, wide, proj, vec):
+    depth = n // 8
+    lead = (depth, 2, 2, 2)
+    copies = 4 * (depth - 1 + 3 * depth + 4)
+    out = tuple(jax.ShapeDtypeStruct(lead + part.shape, part.dtype) for part in (wide, proj, vec))
+    space = pl.BlockSpec(memory_space=pl.ANY)
+    wide_out, proj_out, vec_out = pl.pallas_call(
+        functools.partial(gather_kernel, n),
+        out_shape=out,
+        in_specs=[space] * 3,
+        out_specs=(space,) * 3,
+        scratch_shapes=[
+            pltpu.SemaphoreType.DMA((3,)),
+            pltpu.SemaphoreType.DMA((copies,)),
+            pltpu.SemaphoreType.DMA((copies,)),
+        ],
+        compiler_params=pltpu.CompilerParams(collective_id=0, has_side_effects=True),
+    )(wide, proj, vec)
+    return (
+        wide_out.reshape(n * wide.shape[0], wide.shape[1]),
+        proj_out.reshape(n * proj.shape[0], proj.shape[1]),
+        vec_out.reshape(n, *vec.shape),
+    )
+
+
+def scatter_kernel(
+    n,
+    in_a,
+    att_a,
+    sec_a,
+    sec_b,
+    hid_b,
+    qkv_g,
+    res_g,
+    pre_g,
+    cot,
+    vec,
+    wide_out,
+    proj_out,
+    vec_out,
+    given,
+    kept,
+    land_core,
+    land_second,
+    land_third,
+    land_z,
+    vec_kept,
+    vec_core,
+    vec_second,
+    vec_third,
+    vec_z,
+    ssem,
+    rsem,
+):
+    depth, z, y, x, c = position(n)
+    z_devices = [device_at((z + d) % depth, y, x, c) for d in range(1, depth)]
+    y_peer, x_peer = device_at(z, 1 - y, x, c), device_at(z, y, 1 - x, c)
+    core_peer = device_at(z, y, x, 1 - c)
+    greet(z_devices + [y_peer, x_peer, core_peer])
+    second_peer = (x_peer, y_peer)
+    third_peer = (y_peer, x_peer)
+    spots = ((x, y), (y, x))
+    sends = []
+    count = [8]
+
+    def push(src, dst, device):
+        k = count[0]
+        count[0] = k + 1
+        copy = remote(src, dst, ssem.at[k], rsem.at[k], device)
+        copy.start()
+        sends.append(copy)
+        return copy
+
+    vec_copy = push(vec.at[1 - c], vec_core, core_peer)
+
+    def product(left, right):
+        return jnp.dot(left, right, preferred_element_type=jnp.float32)
+
+    def block(left, right):
+        return product(left, right).reshape(depth, GROUP, D)
+
+    def fill(s, half, t, target):
+        i = (spots[s][0] + 1 - t // 2) % 2
+        j = (spots[s][1] + 1 - t % 2) % 2
+        if s == 0:
+            left = in_a[half, i, j]
+            target[:, 0:48, :] = jnp.concatenate(
+                [block(left, qkv_g[:, 0:D]), block(left, qkv_g[:, D : 2 * D])], axis=1
+            ).astype(jnp.bfloat16)
+            target[:, 48:96, :] = jnp.concatenate(
+                [
+                    block(left, qkv_g[:, 2 * D : 3 * D]),
+                    block(att_a[half, i, j], res_g[...]),
+                ],
+                axis=1,
+            ).astype(jnp.bfloat16)
+            left = sec_a[half, i, j]
+            target[:, 96:144, :] = jnp.concatenate(
+                [block(left, pre_g[:, 0:D]), block(left, pre_g[:, D : 2 * D])], axis=1
+            ).astype(jnp.bfloat16)
+        else:
+            left = sec_b[half, i, j]
+            target[:, 0:48, :] = jnp.concatenate(
+                [block(left, pre_g[:, 2 * D : 3 * D]), block(left, pre_g[:, 3 * D : 4 * D])],
+                axis=1,
+            ).astype(jnp.bfloat16)
+            target[:, 48:144, :] = (
+                product(hid_b[half, i, j], cot[...]).reshape(depth, 96, D).astype(jnp.bfloat16)
+            )
+
+    def core_copy(s, t):
+        k = s * 4 + t
+        return remote(given.at[s, t], land_core.at[s, t], ssem.at[k], rsem.at[k], core_peer)
+
+    def give(t, carry):
+        for s in range(2):
+            fill(s, 1 - c, t, given.at[s, t])
+            core_copy(s, t).start()
+        return carry
+
+    lax.fori_loop(0, 4, give, 0)
+
+    def keep(t, carry):
+        for s in range(2):
+            fill(s, c, t, kept.at[s, t])
+        return carry
+
+    lax.fori_loop(0, 4, keep, 0)
+
+    def merge(target, landed):
+        def step(k, carry):
+            target[k] = (
+                target[k].astype(jnp.float32) + landed[k].astype(jnp.float32)
+            ).astype(jnp.bfloat16)
+            return carry
+
+        lax.fori_loop(0, depth, step, 0)
+
+    vec_copy.wait_recv()
+    vec_kept[...] = vec[c] + vec_core[...]
+    vec_copy = push(vec_kept.at[1 - x], vec_second, x_peer)
+    second = [[], []]
+    for t in range(2):
+        for s in range(2):
+            core_copy(s, t).wait_recv()
+            merge(kept.at[s, t], land_core.at[s, t])
+            second[s].append(push(kept.at[s, t], land_second.at[s, t], second_peer[s]))
+    for t in range(2, 4):
+        for s in range(2):
+            core_copy(s, t).wait_recv()
+            merge(kept.at[s, t], land_core.at[s, t])
+    vec_copy.wait_recv()
+    vec_kept[x] += vec_second[...]
+    vec_copy = push(vec_kept.at[x, 1 - y], vec_third, y_peer)
+    third = []
+    for s in range(2):
+        second[s][0].wait_recv()
+        merge(kept.at[s, 2], land_second.at[s, 0])
+        third.append(push(kept.at[s, 2], land_third.at[s], third_peer[s]))
+    for s in range(2):
+        second[s][1].wait_recv()
+        merge(kept.at[s, 3], land_second.at[s, 1])
+    vec_copy.wait_recv()
+    vec_kept[x, y] += vec_third[...]
+    vec_last = [
+        push(vec_kept.at[x, y, (z + d) % depth], vec_z.at[d - 1], z_devices[d - 1])
+        for d in range(1, depth)
+    ]
+    last = [[], []]
+    for s in range(2):
+        third[s].wait_recv()
+        merge(kept.at[s, 3], land_third.at[s])
+        for d in range(1, depth):
+            last[s].append(
+                push(kept.at[s, 3, (z + d) % depth], land_z.at[s, d - 1], z_devices[d - 1])
+            )
+    total = vec_kept[x, y, z]
+    for d in range(depth - 1):
+        vec_last[d].wait_recv()
+        total += vec_z[d]
+    vec_out[...] = total
+    for s in range(2):
+        for d in range(depth - 1):
+            last[s][d].wait_recv()
+        total = kept[s, 3, z].astype(jnp.float32)
+        for d in range(depth - 1):
+            total += land_z[s, d].astype(jnp.float32)
+        if s == 0:
+            for b in range(6):
+                wide_out[:, b * D : (b + 1) * D] = total[b * GROUP : (b + 1) * GROUP]
+        else:
+            for b in range(2):
+                wide_out[:, (6 + b) * D : (7 + b) * D] = total[b * GROUP : (b + 1) * GROUP]
+            proj_out[...] = total[2 * GROUP :]
+    for s in range(2):
+        for t in range(4):
+            core_copy(s, t).wait_send()
+    for copy in sends:
+        copy.wait_send()
+
+
+def by_owner(rows, n, order):
+    depth = n // 8
+    size = rows.shape[0] // n
+    names = {"y": 1, "x": 2, "c": 3}
+    split = rows.reshape(depth, 2, 2, 2, size, *rows.shape[1:])
+    rest = tuple(range(4, split.ndim))
+    return split.transpose(*(names[k] for k in order), 0, *rest)
+
+
+def scatter_all(n, first_in, attended, second_in, hidden, qkv_grad, resid_half, pre_grad, cot, vec):
+    depth = n // 8
+
+    def left(rows, order):
+        ordered = by_owner(rows.T, n, order)
+        return ordered.reshape(2, 2, 2, -1, rows.shape[0])
+
+    dtype = jnp.bfloat16
+    unit = (depth, 6 * GROUP, D)
+    tile = vec.shape[1:]
+    copies = 8 + 2 * (2 + 1 + depth - 1) + 3 + depth - 1
+    space = pl.BlockSpec(memory_space=pltpu.VMEM)
+    return pl.pallas_call(
+        functools.partial(scatter_kernel, n),
+        out_shape=(
+            jax.ShapeDtypeStruct((GROUP, 8 * D), jnp.float32),
+            jax.ShapeDtypeStruct((4 * GROUP, D), jnp.float32),
+            jax.ShapeDtypeStruct(tile, jnp.float32),
+        ),
+        in_specs=[space] * 10,
+        out_specs=(space,) * 3,
+        scratch_shapes=[
+            pltpu.VMEM((2, 4) + unit, dtype),
+            pltpu.VMEM((2, 4) + unit, dtype),
+            pltpu.VMEM((2, 4) + unit, dtype),
+            pltpu.VMEM((2, 2) + unit, dtype),
+            pltpu.VMEM((2,) + unit, dtype),
+            pltpu.VMEM((2, depth - 1, 6 * GROUP, D), dtype),
+            pltpu.VMEM((2, 2, depth) + tile, jnp.float32),
+            pltpu.VMEM((2, 2, depth) + tile, jnp.float32),
+            pltpu.VMEM((2, depth) + tile, jnp.float32),
+            pltpu.VMEM((depth,) + tile, jnp.float32),
+            pltpu.VMEM((depth - 1,) + tile, jnp.float32),
+            pltpu.SemaphoreType.DMA((copies,)),
+            pltpu.SemaphoreType.DMA((copies,)),
+        ],
+        compiler_params=pltpu.CompilerParams(
+            collective_id=1, has_side_effects=True, vmem_limit_bytes=52 * 2**20
+        ),
+    )(
+        left(first_in, "cxy"),
+        left(attended, "cxy"),
+        left(second_in, "cxy"),
+        left(second_in, "cyx"),
+        left(hidden, "cyx"),
+        qkv_grad,
+        resid_half,
+        pre_grad,
+        cot,
+        by_owner(vec, n, "cxy").reshape(2, 2, 2, depth, *tile),
+    )
+
+
+def to_tile(rows):
+    flat = rows.reshape(rows.shape[0], -1)
+    return jnp.pad(flat, ((0, 0), (0, 1024 - flat.shape[1]))).reshape(rows.shape[0], 8, 128)
+
+
+def from_tile(tiles, rows, columns):
+    return tiles.reshape(tiles.shape[0], 1024)[:, : rows * columns].reshape(-1, rows, columns)
 
 
 def body(
@@ -147,11 +551,24 @@
         proj_weights.astype(jnp.bfloat16),
         vector_params.astype(jnp.bfloat16),
     )
-    wide_full, proj_full, vector_full = (
-        lax.all_gather(shards[0], "fsdp", axis=0, tiled=True),
-        lax.all_gather(shards[1], "fsdp", axis=0, tiled=True),
-        lax.all_gather(shards[2], "fsdp", axis=1, tiled=True),
-    )
+    devices = lax.axis_size("fsdp")
+    direct = wide_weights.shape[0] == GROUP and devices % 8 == 0
+    vector_rows, vector_columns = vector_params.shape
+    if direct:
+        wide_full, proj_full, vector_tiles = gather_all(
+            devices, shards[0], shards[1], to_tile(shards[2].astype(jnp.float32)[None])[0]
+        )
+        vector_full = (
+            from_tile(vector_tiles, vector_rows, vector_columns)
+            .transpose(1, 0, 2)
+            .reshape(vector_rows, devices * vector_columns)
+        )
+    else:
+        wide_full, proj_full, vector_full = (
+            lax.all_gather(shards[0], "fsdp", axis=0, tiled=True),
+            lax.all_gather(shards[1], "fsdp", axis=0, tiled=True),
+            lax.all_gather(shards[2], "fsdp", axis=1, tiled=True),
+        )
     vectors = vector_full.astype(jnp.float32)
     row_count = tokens.shape[0]
     allowed = allowed_pairs(seq_lengths[0], row_count)
@@ -187,11 +604,7 @@
     block_output = (
         residual + jnp.dot(hidden, proj_full, preferred_element_type=jnp.float32) + proj_bias
     ).astype(jnp.bfloat16)
-    backward_wide, backward_proj, vector_again = (
-        lax.all_gather(shards[0], "fsdp", axis=0, tiled=True),
-        lax.all_gather(shards[1], "fsdp", axis=0, tiled=True),
-        lax.all_gather(shards[2], "fsdp", axis=1, tiled=True),
-    )
+    backward_wide, backward_proj, vector_again = wide_full, proj_full, vector_full
     backward_vectors = vector_again.astype(jnp.float32)
     qkv_back = backward_wide[:, : 3 * D]
     out_back = backward_wide[:, 3 * D : 4 * D]
@@ -231,28 +644,44 @@
     attn_vectors = jnp.stack(
         [gain_one_grad, shift_one_grad, query_bias_grad, value_bias_grad, out_bias_grad]
     )
-    fc_part = column_term(second_in, pre_grad)
-    proj_part = column_term(hidden, cotangent).reshape(
-        local_rows * lax.axis_size("fsdp"), ratio * D
-    )
-    qkv_part = column_term(first_in, qkv_grad)
-    out_part = column_term(attended, resid_half)
-    joined_shard = lax.psum_scatter(
-        jnp.concatenate(
-            [
-                jnp.concatenate([qkv_part, out_part], axis=1),
-                jnp.concatenate([fc_part, proj_part], axis=1),
-            ],
-            axis=1,
-        ),
-        "fsdp",
-        scatter_dimension=0,
-        tiled=True,
-    )
-    wide_grad = joined_shard[:, : 4 * D + FF]
-    proj_grad = joined_shard[:, 4 * D + FF :].reshape(local_rows * ratio, D)
     vector_terms = jnp.concatenate([attn_vectors, mlp_vectors], axis=0)
-    vector_grad = lax.psum_scatter(vector_terms, "fsdp", scatter_dimension=1, tiled=True)
+    if direct:
+        owned = vector_terms.reshape(vector_rows, devices, vector_columns).transpose(1, 0, 2)
+        wide_grad, proj_grad, vector_tile = scatter_all(
+            devices,
+            first_in,
+            attended,
+            second_in,
+            hidden,
+            qkv_grad,
+            resid_half,
+            pre_grad,
+            cotangent,
+            to_tile(owned),
+        )
+        vector_grad = from_tile(vector_tile[None], vector_rows, vector_columns)[0]
+    else:
+        fc_part = column_term(second_in, pre_grad)
+        proj_part = column_term(hidden, cotangent).reshape(
+            local_rows * lax.axis_size("fsdp"), ratio * D
+        )
+        qkv_part = column_term(first_in, qkv_grad)
+        out_part = column_term(attended, resid_half)
+        joined_shard = lax.psum_scatter(
+            jnp.concatenate(
+                [
+                    jnp.concatenate([qkv_part, out_part], axis=1),
+                    jnp.concatenate([fc_part, proj_part], axis=1),
+                ],
+                axis=1,
+            ),
+            "fsdp",
+            scatter_dimension=0,
+            tiled=True,
+        )
+        wide_grad = joined_shard[:, : 4 * D + FF]
+        proj_grad = joined_shard[:, 4 * D + FF :].reshape(local_rows * ratio, D)
+        vector_grad = lax.psum_scatter(vector_terms, "fsdp", scatter_dimension=1, tiled=True)
     wide_new, wide_moments_new = adam_update(
         wide_weights, wide_moments, wide_grad, rate_matrix, weight_decay, unscale
     )

time: 504 us -> 252 us (0.50)
  waiting for transfers between devices: 298 us -> 0 us
  Pallas kernels: 0 us -> 191 us
  blocking collectives: 84.7 us -> 0 us
  other arithmetic: 36 us -> 15.8 us
  matrix products: 47.3 us -> 30.7 us
  between operations: 14.3 us -> 1.48 us
  local copies, waits for them, and re-layouts: 22.4 us -> 10.4 us
    reduce_scatter x1 -> x0, waiting for transfers between devices: 203 us -> none  [body(): lax.psum_scatter(jnp.concatenate([jnp.concatenate([qkv_part, out_part], a...]
    pallas_call x0 -> x2, Pallas kernels: none -> 191 us  [the longest x1 115 us: scatter_all(): pl.pallas_call(functools.partial(scatter_kernel, n), out_shape=(jax.Shape...]
    all_gather x2 -> x0, waiting for transfers between devices: 94.7 us -> none  [the longest x1 55.9 us: body(): lax.all_gather(shards[1], 'fsdp', axis=0, tiled=True)]
    all_gather x1 -> x0, blocking collectives: 44.3 us -> none  [body(): lax.all_gather(shards[2], 'fsdp', axis=1, tiled=True)]
    unnamed x1 -> x0, blocking collectives: 40.4 us -> none
    concatenate x1, other arithmetic: 19.5 us -> 0.85 us  [attention_backward(): jnp.concatenate([query_grad.reshape(row_total, D), key_grad.reshape(row_t...]
    dot_general x4 -> x0, matrix products: 15.8 us -> none  [column_term(): jnp.einsum('tc,te->ce', left, right, preferred_element_type=jnp.float32)]
    reshape x3, local copies, waits for them, and re-layouts: 12.3 us -> 0.45 us  [the longest x1 0.15 us: attention_backward(): value_grad.reshape(row_total, D)]
  transfers between devices with their start and end apart: 3 -> 0, of which waited for: 3 -> 0; matrix products, arithmetic and copies ran while one was open for 6% -> 0% of each run, Pallas kernels for 0% -> 0%
where the time goes in v1:
time: 252 us; the launch traced here: 249 us
  Pallas kernels  191 us (76%)
  matrix products  30.7 us (12%)
  other arithmetic  15.8 us (6%)
  local copies, waits for them, and re-layouts  10.4 us (4%)
    pallas_call x1, Pallas kernels, scatter_all(): pl.pallas_call(functools.partial(scatter_kernel, n), out_shape=(jax.Shape...  115 us
    pallas_call x1, Pallas kernels, gather_all(): pl.pallas_call(functools.partial(gather_kernel, n), out_shape=out, in_spe...  75.2 us
    dot_general x1, matrix products, body(): jnp.einsum('td,fd->tf', cotangent, backward_proj, preferred_element_type=...  5.36 us
    another operation x5, other arithmetic, adam_update(): return (updated, jnp.stack([first_moment, second_moment]))  5.34 us

profile of v1, /device:TPU:0, one launch (start us, length us, event | category | flops | bytes accessed | tf_op | source)
XLA Modules:
  0.0 248.9 jit_solution(12551019699870186438)
XLA Ops:
  0.7 1.8 convert_element_type.80.wide
  2.5 1.6 convert_element_type.81.proj
  4.1 0.7 convert_element_type.82
  4.9 0.6 pad_convert_fusion
  5.5 75.2 %shard_map.176 = (bf16[4,2,2,2,24,6144]{5,4,3,2,1,0:T(8,128)(2,1)}, bf16[4,2,2,2,96,768]{5,4,3,2,1,0:T(8,128)(2,1)}, f32[4,2,2,2,8,128]{5,4,3,2,1,0:T(8,128)}) custom-call(bf16[24,6144]{1,0:T(8,128)(2,1)} %convert_element_type.80.wide, bf16[96,768]{1,0:T(8,128)(2,1)} %convert_element_type.81.proj, f32[8,128]{1,0:T(8,128)} %bitcast.192), custom_call_target="tpu_custom_call" | custom-call | tf_op jit(solution)/shard_map/pallas_call | solution.py:272
  80.8 0.9 copy.155
  83.0 2.7 %fusion.10 = bf16[128,2304]{1,0:T(8,128)(2,1)S(1)} fusion(bf16[768,6144]{1,0:T(8,128)(2,1)} %bitcast.183, f32[2304]{0:T(1024)S(1)} %pad_maximum_fusion.4, bf16[128,768]{1,0:T(8,128)(2,1)S(1)} %copy-done.1, f32[768]{0:T(1024)S(1)} %add.173, f32[768]{0:T(1024)S(1)} %mul.346, f32[128]{0:T(128)S(1)} %add_rsqrt_fusion.1, f32[128]{0:T(128)S(1)} %broadcast_multiply_fusion.5), kind=kOutput, calls=%fused_computation.10 | convolution fusion | flops 454164480 | bytes 4341760 | tf_op jit(solution)/shard_map/dot_general | solution.py:586
  87.5 1.7 fusion.101
  90.0 5.0 %fusion.23 = (bf16[3072,128]{0,1:T(8,128)(2,1)}, f32[128,3072]{1,0:T(8,128)}) fusion(f32[3072]{0:T(1024)S(1)} %add.187, bf16[768,6144]{1,0:T(8,128)(2,1)} %bitcast.185, f32[128,768]{1,0:T(8,128)S(1)} %get-tuple-element.83, f32[768]{0:T(1024)S(1)} %add.184, f32[768]{0:T(1024)S(1)} %mul.353, f32[128]{0:T(128)S(1)} %add_rsqrt_fusion, ...), kind=kOutput, calls=%fused_computation.26 | convolution fusion | flops 608403456 | bytes 7490560 | tf_op jit(solution)/shard_map/dot_general | solution.py:600
  95.2 4.7 %fusion.31 = bf16[128,768]{1,0:T(8,128)(2,1)} fusion(f32[128,768]{1,0:T(8,128)S(1)} %get-tuple-element.83, bf16[3072,768]{1,0:T(8,128)(2,1)} %bitcast.193, f32[128,3072]{1,0:T(8,128)} %get-tuple-element.85, f32[768]{0:T(1024)S(1)} %add.193), kind=kOutput, calls=%fused_computation.41 | convolution fusion | flops 607813632 | bytes 6884352 | tf_op jit(solution)/shard_map/dot_general | solution.py:605
  99.9 5.4 %convert_reduce_fusion = (f32[3072]{0:T(1024)}, bf16[128,3072]{1,0:T(8,128)(2,1)S(1)}) fusion(f32[128,3072]{1,0:T(8,128)} %get-tuple-element.85, bf16[3072,768]{1,0:T(8,128)(2,1)} %bitcast.194, bf16[128,768]{1,0:T(8,128)(2,1)S(1)} %copy-done), kind=kOutput, calls=%fused_computation.28 | convolution fusion | flops 612234240 | bytes 7286784 | tf_op jit(solution)/shard_map/td,fd->tf/dot_general | solution.py:614
  105.3 1.7 fusion.1
  107.0 0.8 multiply_reduce_fusion.1
  107.8 0.8 fusion.96
  108.6 0.5 convolution_convert_fusion.3
  109.9 1.2 fusion.102
  111.1 1.8 convolution_convert_fusion.1
  113.0 1.7 convolution_convert_fusion.2
  115.0 3.3 %fusion.11 = f32[128,768]{1,0:T(8,128)S(1)} fusion(bf16[768,6144]{1,0:T(8,128)(2,1)} %bitcast.186, bf16[128,768]{1,0:T(8,128)(2,1)S(1)} %copy.96, bf16[128,768]{1,0:T(8,128)(2,1)S(1)} %copy.95, bf16[128,768]{1,0:T(8,128)(2,1)S(1)} %copy.94), kind=kOutput, calls=%fused_computation.11 | convolution fusion | flops 454754304 | bytes 4521984 | tf_op jit(solution)/shard_map/tc,dc->td/dot_general | solution.py:639
  118.6 0.9 fusion.55
  120.1 1.5 copy.103
  121.6 0.9 copy.104
  122.6 0.9 pad_maximum_fusion.1.qkv_g
  125.0 115.4 %shard_map.177 = (f32[24,6144]{1,0:T(8,128)}, f32[96,768]{1,0:T(8,128)S(1)}, f32[8,128]{1,0:T(8,128)S(1)}) custom-call(bf16[2,2,2,96,128]{4,3,2,1,0:T(8,128)(2,1)S(1)} %bitcast.153, bf16[2,2,2,96,128]{4,3,2,1,0:T(8,128)(2,1)S(1)} %bitcast.154, bf16[2,2,2,96,128]{4,3,2,1,0:T(8,128)(2,1)S(1)} %bitcast.155, bf16[2,2,2,96,128]{4,3,2,1,0:T(8,128)(2,1)S(1)} %bitcast.156, ...), custom_call_target="tpu_custom_call" | custom-call | tf_op jit(solution)/shard_map/pallas_call | solution.py:488
  240.6 2.4 fusion.64
  243.0 1.0 fusion.68
  244.0 0.6 fusion.80
  244.7 1.1 pad_maximum_fusion
  245.7 0.9 pad_maximum_fusion.2
  246.8 0.6 copy.110
  247.4 0.8 copy.167
  248.2 0.7 copy.168
  (141 shorter events, 7.5 us)
Async XLA Ops:
  0.6 82.0 %copy-start.1 = (bf16[128,768]{1,0:T(8,128)(2,1)S(1)}, bf16[128,768]{1,0:T(8,128)(2,1)}, u32[]{:S(2)}) copy-start(bf16[128,768]{1,0:T(8,128)(2,1)} %param.9) | copy-start | bytes 589828
  82.8 2.9 %copy-start.16 = (f32[128]{0:T(128)}, f32[128]{0:T(128)S(1)}, u32[]{:S(2)}) copy-start(f32[128]{0:T(128)S(1)} %broadcast_multiply_fusion.5) | copy-start | bytes 1540
  83.0 2.7 %copy-start.18 = (f32[128]{0:T(128)}, f32[128]{0:T(128)S(1)}, u32[]{:S(2)}) copy-start(f32[128]{0:T(128)S(1)} %add_rsqrt_fusion.1) | copy-start | bytes 1540
  85.8 0.7 copy-start.20
  95.2 4.7 %copy-start = (bf16[128,768]{1,0:T(8,128)(2,1)S(1)}, bf16[128,768]{1,0:T(8,128)(2,1)}, u32[]{:S(2)}) copy-start(bf16[128,768]{1,0:T(8,128)(2,1)} %cot.1) | copy-start | bytes 589828
  95.2 10.1 %slice-start = ((s8[9437184]{0:T(1024)(128)(4,1)}), s8[4194304]{0:T(1024)(128)(4,1)S(1)}, s32[]{:S(2)}) async-start(s8[9437184]{0:T(1024)(128)(4,1)} %bitcast.187), calls=%async_computation | async-start | bytes 8388608
  95.2 10.1 %slice-start.1 = ((s8[9437184]{0:T(1024)(128)(4,1)}), s8[4194304]{0:T(1024)(128)(4,1)S(1)}, s32[]{:S(2)}) async-start(s8[9437184]{0:T(1024)(128)(4,1)} %bitcast.187), calls=%async_computation.1 | async-start | bytes 8388608
  99.9 5.4 %slice-start.2 = ((s8[9437184]{0:T(1024)(128)(4,1)}), s8[1048576]{0:T(1024)(128)(4,1)S(1)}, s32[]{:S(2)}) async-start(s8[9437184]{0:T(1024)(128)(4,1)} %bitcast.187), calls=%async_computation.2 | async-start | bytes 2097152
  105.3 1.7 copy-start.6
  114.9 3.3 %copy-start.17 = (f32[128]{0:T(128)S(1)}, f32[128]{0:T(128)}, u32[]{:S(2)}) copy-start(f32[128]{0:T(128)} %copy-done.16) | copy-start | bytes 1540
  115.0 3.3 %copy-start.19 = (f32[128]{0:T(128)S(1)}, f32[128]{0:T(128)}, u32[]{:S(2)}) copy-start(f32[128]{0:T(128)} %copy-done.18) | copy-start | bytes 1540
  121.6 2.6 %copy-start.13 = (f32[768]{0:T(1024)S(1)}, f32[768]{0:T(1024)}, u32[]{:S(2)}) copy-start(f32[768]{0:T(1024)} %get-tuple-element.56) | copy-start | bytes 9220
  121.6 2.7 %copy-start.11 = (f32[768]{0:T(1024)S(1)}, f32[768]{0:T(1024)}, u32[]{:S(2)}) copy-start(f32[768]{0:T(1024)} %get-tuple-element.45) | copy-start | bytes 9220
  121.6 2.8 %copy-start.10 = (f32[768]{0:T(1024)S(1)}, f32[768]{0:T(1024)}, u32[]{:S(2)}) copy-start(f32[768]{0:T(1024)} %get-tuple-element.51) | copy-start | bytes 9220
  121.6 2.8 %copy-start.12 = (f32[768]{0:T(1024)S(1)}, f32[768]{0:T(1024)}, u32[]{:S(2)}) copy-start(f32[768]{0:T(1024)} %get-tuple-element.69) | copy-start | bytes 9220
  121.6 2.9 %copy-start.14 = (f32[3072]{0:T(1024)S(1)}, f32[3072]{0:T(1024)}, u32[]{:S(2)}) copy-start(f32[3072]{0:T(1024)} %get-tuple-element.86) | copy-start | bytes 36868
  125.0 115.5 %copy-start.2 = (f32[24,6144]{1,0:T(8,128)S(1)}, f32[24,6144]{1,0:T(8,128)}, u32[]{:S(2)}) copy-start(f32[24,6144]{1,0:T(8,128)} %param.12) | copy-start | bytes 1769476
  125.0 115.5 %copy-start.5 = (f32[2,24,6144]{2,1,0:T(8,128)S(1)}, f32[2,24,6144]{2,1,0:T(8,128)}, u32[]{:S(2)}) copy-start(f32[2,24,6144]{2,1,0:T(8,128)} %param.15) | copy-start | bytes 3538948
  240.6 3.5 %copy-start.8 = (f32[12,24]{1,0:T(8,128)}, f32[12,24]{1,0:T(8,128)S(1)}, u32[]{:S(2)}) copy-start(f32[12,24]{1,0:T(8,128)S(1)} %squeeze_reshape.10) | copy-start | bytes 3460
  240.6 2.5 copy-start.4
  240.6 2.4 copy-start.7
  243.0 1.0 copy-start.15
  243.0 1.0 copy-start.9
  244.7 2.8 %copy-start.3 = (f32[24,6144]{1,0:T(8,128)S(1)}, f32[24,6144]{1,0:T(8,128)}, u32[]{:S(2)}) copy-start(f32[24,6144]{1,0:T(8,128)} %get-tuple-element.103) | copy-start | bytes 1769476

commit v2 on v1

--- a/solution.py
+++ b/solution.py
@@ -326,7 +326,7 @@
     third_peer = (y_peer, x_peer)
     spots = ((x, y), (y, x))
     sends = []
-    count = [8]
+    count = [24]
 
     def push(src, dst, device):
         k = count[0]
@@ -344,53 +344,51 @@
     def block(left, right):
         return product(left, right).reshape(depth, GROUP, D)
 
-    def fill(s, half, t, target):
+    def fill(k, s, half, t, target):
         i = (spots[s][0] + 1 - t // 2) % 2
         j = (spots[s][1] + 1 - t % 2) % 2
         if s == 0:
             left = in_a[half, i, j]
-            target[:, 0:48, :] = jnp.concatenate(
-                [block(left, qkv_g[:, 0:D]), block(left, qkv_g[:, D : 2 * D])], axis=1
-            ).astype(jnp.bfloat16)
-            target[:, 48:96, :] = jnp.concatenate(
-                [
+            if k == 0:
+                pair = (block(left, qkv_g[:, 0:D]), block(left, qkv_g[:, D : 2 * D]))
+            elif k == 1:
+                pair = (
                     block(left, qkv_g[:, 2 * D : 3 * D]),
                     block(att_a[half, i, j], res_g[...]),
-                ],
-                axis=1,
-            ).astype(jnp.bfloat16)
-            left = sec_a[half, i, j]
-            target[:, 96:144, :] = jnp.concatenate(
-                [block(left, pre_g[:, 0:D]), block(left, pre_g[:, D : 2 * D])], axis=1
-            ).astype(jnp.bfloat16)
+                )
+            else:
+                left = sec_a[half, i, j]
+                pair = (block(left, pre_g[:, 0:D]), block(left, pre_g[:, D : 2 * D]))
+            value = jnp.concatenate(pair, axis=1)
+        elif k == 0:
+            left = sec_b[half, i, j]
+            value = jnp.concatenate(
+                (block(left, pre_g[:, 2 * D : 3 * D]), block(left, pre_g[:, 3 * D : 4 * D])), axis=1
+            )
         else:
-            left = sec_b[half, i, j]
-            target[:, 0:48, :] = jnp.concatenate(
-                [block(left, pre_g[:, 2 * D : 3 * D]), block(left, pre_g[:, 3 * D : 4 * D])],
-                axis=1,
-            ).astype(jnp.bfloat16)
-            target[:, 48:144, :] = (
-                product(hid_b[half, i, j], cot[...]).reshape(depth, 96, D).astype(jnp.bfloat16)
-            )
-
-    def core_copy(s, t):
-        k = s * 4 + t
-        return remote(given.at[s, t], land_core.at[s, t], ssem.at[k], rsem.at[k], core_peer)
-
-    def give(t, carry):
-        for s in range(2):
-            fill(s, 1 - c, t, given.at[s, t])
-            core_copy(s, t).start()
-        return carry
-
-    lax.fori_loop(0, 4, give, 0)
-
-    def keep(t, carry):
-        for s in range(2):
-            fill(s, c, t, kept.at[s, t])
-        return carry
-
-    lax.fori_loop(0, 4, keep, 0)
+            value = product(hid_b[k - 1, half, i, j], cot[...]).reshape(depth, 2 * GROUP, D)
+        target[...] = value.astype(jnp.bfloat16)
+
+    def core_copy(k, s, t):
+        q = (k * 2 + s) * 4 + t
+        return remote(
+            given.at[k, s, t], land_core.at[k, s, t], ssem.at[q], rsem.at[q], core_peer
+        )
+
+    def multiply(k):
+        def give(t, carry):
+            for s in range(2):
+                fill(k, s, 1 - c, t, given.at[k, s, t])
+                core_copy(k, s, t).start()
+            return carry
+
+        def keep(t, carry):
+            for s in range(2):
+                fill(k, s, c, t, kept.at[k, s, t])
+            return carry
+
+        lax.fori_loop(0, 4, give, 0)
+        lax.fori_loop(0, 4, keep, 0)
 
     def merge(target, landed):
         def step(k, carry):
@@ -401,65 +399,85 @@
 
         lax.fori_loop(0, depth, step, 0)
 
+    second, third, last = {}, {}, {}
+
+    def stage_second(k):
+        for t in range(4):
+            for s in range(2):
+                core_copy(k, s, t).wait_recv()
+                merge(kept.at[k, s, t], land_core.at[k, s, t])
+                if t < 2:
+                    second[k, s, t] = push(
+                        kept.at[k, s, t], land_second.at[k, s, t], second_peer[s]
+                    )
+
+    def stage_third(k):
+        for t in range(2):
+            for s in range(2):
+                second[k, s, t].wait_recv()
+                merge(kept.at[k, s, 2 + t], land_second.at[k, s, t])
+                if t == 0:
+                    third[k, s] = push(kept.at[k, s, 2], land_third.at[k, s], third_peer[s])
+
+    def stage_last(k):
+        for s in range(2):
+            third[k, s].wait_recv()
+            merge(kept.at[k, s, 3], land_third.at[k, s])
+            last[k, s] = [
+                push(kept.at[k, s, 3, (z + d) % depth], land_z.at[k, s, d - 1], z_devices[d - 1])
+                for d in range(1, depth)
+            ]
+
+    def finish(k):
+        for s in range(2):
+            total = kept[k, s, 3, z].astype(jnp.float32)
+            for d in range(depth - 1):
+                last[k, s][d].wait_recv()
+                total += land_z[k, s, d].astype(jnp.float32)
+            for b in range(2):
+                rows = total[b * GROUP : (b + 1) * GROUP]
+                if s == 1 and k > 0:
+                    first = ((k - 1) * 2 + b) * GROUP
+                    proj_out[first : first + GROUP] = rows
+                else:
+                    column = (6 * s + 2 * k + b) * D
+                    wide_out[:, column : column + D] = rows
+
+    multiply(0)
+    stage_second(0)
     vec_copy.wait_recv()
     vec_kept[...] = vec[c] + vec_core[...]
     vec_copy = push(vec_kept.at[1 - x], vec_second, x_peer)
-    second = [[], []]
-    for t in range(2):
-        for s in range(2):
-            core_copy(s, t).wait_recv()
-            merge(kept.at[s, t], land_core.at[s, t])
-            second[s].append(push(kept.at[s, t], land_second.at[s, t], second_peer[s]))
-    for t in range(2, 4):
-        for s in range(2):
-            core_copy(s, t).wait_recv()
-            merge(kept.at[s, t], land_core.at[s, t])
+    multiply(1)
+    stage_second(1)
+    stage_third(0)
     vec_copy.wait_recv()
     vec_kept[x] += vec_second[...]
     vec_copy = push(vec_kept.at[x, 1 - y], vec_third, y_peer)
-    third = []
-    for s in range(2):
-        second[s][0].wait_recv()
-        merge(kept.at[s, 2], land_second.at[s, 0])
-        third.append(push(kept.at[s, 2], land_third.at[s], third_peer[s]))
-    for s in range(2):
-        second[s][1].wait_recv()
-        merge(kept.at[s, 3], land_second.at[s, 1])
+    multiply(2)
+    stage_second(2)
+    stage_last(0)
+    stage_third(1)
     vec_copy.wait_recv()
     vec_kept[x, y] += vec_third[...]
     vec_last = [
         push(vec_kept.at[x, y, (z + d) % depth], vec_z.at[d - 1], z_devices[d - 1])
         for d in range(1, depth)
     ]
-    last = [[], []]
-    for s in range(2):
-        third[s].wait_recv()
-        merge(kept.at[s, 3], land_third.at[s])
-        for d in range(1, depth):
-            last[s].append(
-                push(kept.at[s, 3, (z + d) % depth], land_z.at[s, d - 1], z_devices[d - 1])
-            )
+    stage_last(1)
+    stage_third(2)
+    stage_last(2)
     total = vec_kept[x, y, z]
     for d in range(depth - 1):
         vec_last[d].wait_recv()
         total += vec_z[d]
     vec_out[...] = total
-    for s in range(2):
-        for d in range(depth - 1):
-            last[s][d].wait_recv()
-        total = kept[s, 3, z].astype(jnp.float32)
-        for d in range(depth - 1):
-            total += land_z[s, d].astype(jnp.float32)
-        if s == 0:
-            for b in range(6):
-                wide_out[:, b * D : (b + 1) * D] = total[b * GROUP : (b + 1) * GROUP]
-        else:
-            for b in range(2):
-                wide_out[:, (6 + b) * D : (7 + b) * D] = total[b * GROUP : (b + 1) * GROUP]
-            proj_out[...] = total[2 * GROUP :]
-    for s in range(2):
-        for t in range(4):
-            core_copy(s, t).wait_send()
+    for k in range(3):
+        finish(k)
+    for k in range(3):
+        for s in range(2):
+            for t in range(4):
+                core_copy(k, s, t).wait_send()
     for copy in sends:
         copy.wait_send()
 
@@ -481,9 +499,9 @@
         return ordered.reshape(2, 2, 2, -1, rows.shape[0])
 
     dtype = jnp.bfloat16
-    unit = (depth, 6 * GROUP, D)
+    unit = (depth, 2 * GROUP, D)
     tile = vec.shape[1:]
-    copies = 8 + 2 * (2 + 1 + depth - 1) + 3 + depth - 1
+    copies = 24 + 6 * (2 + 1 + depth - 1) + 3 + depth - 1
     space = pl.BlockSpec(memory_space=pltpu.VMEM)
     return pl.pallas_call(
         functools.partial(scatter_kernel, n),
@@ -495,12 +513,12 @@
         in_specs=[space] * 10,
         out_specs=(space,) * 3,
         scratch_shapes=[
-            pltpu.VMEM((2, 4) + unit, dtype),
-            pltpu.VMEM((2, 4) + unit, dtype),
-            pltpu.VMEM((2, 4) + unit, dtype),
-            pltpu.VMEM((2, 2) + unit, dtype),
-            pltpu.VMEM((2,) + unit, dtype),
-            pltpu.VMEM((2, depth - 1, 6 * GROUP, D), dtype),
+            pltpu.VMEM((3, 2, 4) + unit, dtype),
+            pltpu.VMEM((3, 2, 4) + unit, dtype),
+            pltpu.VMEM((3, 2, 4) + unit, dtype),
+            pltpu.VMEM((3, 2, 2) + unit, dtype),
+            pltpu.VMEM((3, 2) + unit, dtype),
+            pltpu.VMEM((3, 2, depth - 1, 2 * GROUP, D), dtype),
             pltpu.VMEM((2, 2, depth) + tile, jnp.float32),
             pltpu.VMEM((2, 2, depth) + tile, jnp.float32),
             pltpu.VMEM((2, depth) + tile, jnp.float32),
@@ -517,7 +535,10 @@
         left(attended, "cxy"),
         left(second_in, "cxy"),
         left(second_in, "cyx"),
-        left(hidden, "cyx"),
+        by_owner(hidden.T, n, "cyx")
+        .reshape(2, 2, 2, depth, 2, 2 * GROUP, hidden.shape[0])
+        .transpose(4, 0, 1, 2, 3, 5, 6)
+        .reshape(2, 2, 2, 2, depth * 2 * GROUP, hidden.shape[0]),
         qkv_grad,
         resid_half,
         pre_grad,

time: 252 us -> 231 us (0.917); the launches traced: 249 us -> 231 us
  Pallas kernels: 191 us -> 172 us
    pallas_call x1, Pallas kernels: 115 us -> 97.2 us  [scatter_all(): pl.pallas_call(functools.partial(scatter_kernel, n), out_shape=(jax.Shape...]
where the time goes in v2:
time: 231 us
  Pallas kernels  172 us (74%)
  matrix products  30.7 us (13%)
  other arithmetic  15.8 us (7%)
  local copies, waits for them, and re-layouts  10.4 us (5%)
    pallas_call x1, Pallas kernels, scatter_all(): pl.pallas_call(functools.partial(scatter_kernel, n), out_shape=(jax.Shape...  97.2 us
    pallas_call x1, Pallas kernels, gather_all(): pl.pallas_call(functools.partial(gather_kernel, n), out_shape=out, in_spe...  75.2 us
    dot_general x1, matrix products, body(): jnp.einsum('td,fd->tf', cotangent, backward_proj, preferred_element_type=...  5.36 us
    another operation x5, other arithmetic, adam_update(): return (updated, jnp.stack([first_moment, second_moment]))  5.34 us
    dot_general x1, matrix products, body(): jnp.dot(second_in, wide_full[:, 4 * D:], preferred_element_type=jnp.float32)  5.04 us
    dot_general x1, matrix products, body(): jnp.dot(hidden, proj_full, preferred_element_type=jnp.float32)  4.69 us

profile of v2, /device:TPU:0, one launch (start us, length us, event | category | flops | bytes accessed | tf_op | source)
XLA Modules:
  0.0 230.8 jit_solution(7741233673446574520)
XLA Ops:
  0.7 1.8 convert_element_type.80.wide
  2.5 1.6 convert_element_type.81.proj
  4.1 0.7 convert_element_type.82
  4.9 0.6 pad_convert_fusion
  5.5 75.2 %shard_map.176 = (bf16[4,2,2,2,24,6144]{5,4,3,2,1,0:T(8,128)(2,1)}, bf16[4,2,2,2,96,768]{5,4,3,2,1,0:T(8,128)(2,1)}, f32[4,2,2,2,8,128]{5,4,3,2,1,0:T(8,128)}) custom-call(bf16[24,6144]{1,0:T(8,128)(2,1)} %convert_element_type.80.wide, bf16[96,768]{1,0:T(8,128)(2,1)} %convert_element_type.81.proj, f32[8,128]{1,0:T(8,128)} %bitcast.196), custom_call_target="tpu_custom_call" | custom-call | tf_op jit(solution)/shard_map/pallas_call | solution.py:272
  80.8 0.9 copy.158
  83.0 2.7 %fusion.10 = bf16[128,2304]{1,0:T(8,128)(2,1)S(1)} fusion(bf16[768,6144]{1,0:T(8,128)(2,1)} %bitcast.187, f32[2304]{0:T(1024)S(1)} %pad_maximum_fusion.4, bf16[128,768]{1,0:T(8,128)(2,1)S(1)} %copy-done.1, f32[768]{0:T(1024)S(1)} %add.173, f32[768]{0:T(1024)S(1)} %mul.346, f32[128]{0:T(128)S(1)} %add_rsqrt_fusion.1, f32[128]{0:T(128)S(1)} %broadcast_multiply_fusion.5), kind=kOutput, calls=%fused_computation.10 | convolution fusion | flops 454164480 | bytes 4341760 | tf_op jit(solution)/shard_map/dot_general | solution.py:607
  87.5 1.7 fusion.101
  90.0 5.0 %fusion.23 = (bf16[3072,128]{0,1:T(8,128)(2,1)}, f32[128,3072]{1,0:T(8,128)}) fusion(f32[3072]{0:T(1024)S(1)} %add.187, bf16[768,6144]{1,0:T(8,128)(2,1)} %bitcast.189, f32[128,768]{1,0:T(8,128)S(1)} %get-tuple-element.83, f32[768]{0:T(1024)S(1)} %add.184, f32[768]{0:T(1024)S(1)} %mul.353, f32[128]{0:T(128)S(1)} %add_rsqrt_fusion, ...), kind=kOutput, calls=%fused_computation.26 | convolution fusion | flops 608403456 | bytes 7490560 | tf_op jit(solution)/shard_map/dot_general | solution.py:621
  95.2 4.7 %fusion.31 = bf16[128,768]{1,0:T(8,128)(2,1)} fusion(f32[128,768]{1,0:T(8,128)S(1)} %get-tuple-element.83, bf16[3072,768]{1,0:T(8,128)(2,1)} %bitcast.197, f32[128,3072]{1,0:T(8,128)} %get-tuple-element.85, f32[768]{0:T(1024)S(1)} %add.193), kind=kOutput, calls=%fused_computation.41 | convolution fusion | flops 607813632 | bytes 6884352 | tf_op jit(solution)/shard_map/dot_general | solution.py:626
  99.9 5.4 %convert_reduce_fusion = (f32[3072]{0:T(1024)}, bf16[128,3072]{1,0:T(8,128)(2,1)S(1)}) fusion(f32[128,3072]{1,0:T(8,128)} %get-tuple-element.85, bf16[3072,768]{1,0:T(8,128)(2,1)} %bitcast.198, bf16[128,768]{1,0:T(8,128)(2,1)S(1)} %copy-done), kind=kOutput, calls=%fused_computation.28 | convolution fusion | flops 612234240 | bytes 7286784 | tf_op jit(solution)/shard_map/td,fd->tf/dot_general | solution.py:635
  105.3 1.7 fusion.1
  107.0 0.8 multiply_reduce_fusion.1
  107.8 0.8 fusion.96
  108.6 0.5 convolution_convert_fusion.3
  109.9 1.2 fusion.102
  111.1 1.8 convolution_convert_fusion.1
  113.0 1.7 convolution_convert_fusion.2
  115.0 3.3 %fusion.11 = f32[128,768]{1,0:T(8,128)S(1)} fusion(bf16[768,6144]{1,0:T(8,128)(2,1)} %bitcast.190, bf16[128,768]{1,0:T(8,128)(2,1)S(1)} %copy.97, bf16[128,768]{1,0:T(8,128)(2,1)S(1)} %copy.96, bf16[128,768]{1,0:T(8,128)(2,1)S(1)} %copy.95), kind=kOutput, calls=%fused_computation.11 | convolution fusion | flops 454754304 | bytes 4521984 | tf_op jit(solution)/shard_map/tc,dc->td/dot_general | solution.py:660
  118.6 0.9 fusion.55
  120.1 1.5 copy.104
  121.6 1.0 copy.106
  122.6 0.9 pad_maximum_fusion.1.qkv_g
  125.0 97.2 %shard_map.177 = (f32[24,6144]{1,0:T(8,128)}, f32[96,768]{1,0:T(8,128)S(1)}, f32[8,128]{1,0:T(8,128)S(1)}) custom-call(bf16[2,2,2,96,128]{4,3,2,1,0:T(8,128)(2,1)S(1)} %bitcast.157, bf16[2,2,2,96,128]{4,3,2,1,0:T(8,128)(2,1)S(1)} %bitcast.158, bf16[2,2,2,96,128]{4,3,2,1,0:T(8,128)(2,1)S(1)} %bitcast.159, bf16[2,2,2,96,128]{4,3,2,1,0:T(8,128)(2,1)S(1)} %bitcast.160, ...), custom_call_target="tpu_custom_call" | custom-call | tf_op jit(solution)/shard_map/pallas_call | solution.py:506
  222.4 2.4 %fusion.64 = (f32[1,24,6144]{2,1,0:T(8,128)S(1)}, f32[1,24,6144]{2,1,0:T(8,128)S(1)}, f32[24,6144]{1,0:T(8,128)}) fusion(f32[24,6144]{1,0:T(8,128)} %get-tuple-element.103, f32[2,24,6144]{2,1,0:T(8,128)S(1)} %copy-done.5, f32[24,6144]{1,0:T(8,128)S(1)} %copy-done.2), kind=kLoop, calls=%fused_computation.99 | loop fusion | flops 2359296 | bytes 4128768 | tf_op jit(solution)/shard_map/stack | solution.py:130
  224.9 1.0 fusion.68
  225.9 0.6 fusion.80
  226.5 1.1 pad_maximum_fusion
  227.6 0.9 pad_maximum_fusion.2
  228.6 0.6 copy.112
  229.3 0.8 copy.170
  230.1 0.7 copy.171
  (141 shorter events, 7.5 us)
Async XLA Ops:
  0.6 82.0 %copy-start.1 = (bf16[128,768]{1,0:T(8,128)(2,1)S(1)}, bf16[128,768]{1,0:T(8,128)(2,1)}, u32[]{:S(2)}) copy-start(bf16[128,768]{1,0:T(8,128)(2,1)} %param.9) | copy-start | bytes 589828
  82.8 2.9 %copy-start.16 = (f32[128]{0:T(128)}, f32[128]{0:T(128)S(1)}, u32[]{:S(2)}) copy-start(f32[128]{0:T(128)S(1)} %broadcast_multiply_fusion.5) | copy-start | bytes 1540
  83.0 2.7 %copy-start.18 = (f32[128]{0:T(128)}, f32[128]{0:T(128)S(1)}, u32[]{:S(2)}) copy-start(f32[128]{0:T(128)S(1)} %add_rsqrt_fusion.1) | copy-start | bytes 1540
  85.8 0.7 copy-start.20
  95.2 4.7 %copy-start = (bf16[128,768]{1,0:T(8,128)(2,1)S(1)}, bf16[128,768]{1,0:T(8,128)(2,1)}, u32[]{:S(2)}) copy-start(bf16[128,768]{1,0:T(8,128)(2,1)} %cot.1) | copy-start | bytes 589828
  95.2 10.1 %slice-start = ((s8[9437184]{0:T(1024)(128)(4,1)}), s8[4194304]{0:T(1024)(128)(4,1)S(1)}, s32[]{:S(2)}) async-start(s8[9437184]{0:T(1024)(128)(4,1)} %bitcast.191), calls=%async_computation | async-start | bytes 8388608
  95.2 10.1 %slice-start.1 = ((s8[9437184]{0:T(1024)(128)(4,1)}), s8[4194304]{0:T(1024)(128)(4,1)S(1)}, s32[]{:S(2)}) async-start(s8[9437184]{0:T(1024)(128)(4,1)} %bitcast.191), calls=%async_computation.1 | async-start | bytes 8388608
  99.9 5.4 %slice-start.2 = ((s8[9437184]{0:T(1024)(128)(4,1)}), s8[1048576]{0:T(1024)(128)(4,1)S(1)}, s32[]{:S(2)}) async-start(s8[9437184]{0:T(1024)(128)(4,1)} %bitcast.191), calls=%async_computation.2 | async-start | bytes 2097152
  105.3 1.7 copy-start.6
  114.9 3.3 %copy-start.17 = (f32[128]{0:T(128)S(1)}, f32[128]{0:T(128)}, u32[]{:S(2)}) copy-start(f32[128]{0:T(128)} %copy-done.16) | copy-start | bytes 1540
  115.0 3.3 %copy-start.19 = (f32[128]{0:T(128)S(1)}, f32[128]{0:T(128)}, u32[]{:S(2)}) copy-start(f32[128]{0:T(128)} %copy-done.18) | copy-start | bytes 1540
  121.6 2.6 %copy-start.13 = (f32[768]{0:T(1024)S(1)}, f32[768]{0:T(1024)}, u32[]{:S(2)}) copy-start(f32[768]{0:T(1024)} %get-tuple-element.56) | copy-start | bytes 9220
  121.6 2.7 %copy-start.11 = (f32[768]{0:T(1024)S(1)}, f32[768]{0:T(1024)}, u32[]{:S(2)}) copy-start(f32[768]{0:T(1024)} %get-tuple-element.45) | copy-start | bytes 9220
  121.6 2.8 %copy-start.10 = (f32[768]{0:T(1024)S(1)}, f32[768]{0:T(1024)}, u32[]{:S(2)}) copy-start(f32[768]{0:T(1024)} %get-tuple-element.51) | copy-start | bytes 9220
  121.6 2.9 %copy-start.12 = (f32[768]{0:T(1024)S(1)}, f32[768]{0:T(1024)}, u32[]{:S(2)}) copy-start(f32[768]{0:T(1024)} %get-tuple-element.69) | copy-start | bytes 9220
  121.6 3.0 %copy-start.14 = (f32[3072]{0:T(1024)S(1)}, f32[3072]{0:T(1024)}, u32[]{:S(2)}) copy-start(f32[3072]{0:T(1024)} %get-tuple-element.86) | copy-start | bytes 36868
  125.0 97.4 %copy-start.2 = (f32[24,6144]{1,0:T(8,128)S(1)}, f32[24,6144]{1,0:T(8,128)}, u32[]{:S(2)}) copy-start(f32[24,6144]{1,0:T(8,128)} %param.12) | copy-start | bytes 1769476
  125.0 97.4 %copy-start.5 = (f32[2,24,6144]{2,1,0:T(8,128)S(1)}, f32[2,24,6144]{2,1,0:T(8,128)}, u32[]{:S(2)}) copy-start(f32[2,24,6144]{2,1,0:T(8,128)} %param.15) | copy-start | bytes 3538948
  222.4 3.5 %copy-start.8 = (f32[12,24]{1,0:T(8,128)}, f32[12,24]{1,0:T(8,128)S(1)}, u32[]{:S(2)}) copy-start(f32[12,24]{1,0:T(8,128)S(1)} %squeeze_reshape.10) | copy-start | bytes 3460
  222.4 2.5 %copy-start.4 = (f32[96,768]{1,0:T(8,128)S(1)}, f32[96,768]{1,0:T(8,128)}, u32[]{:S(2)}) copy-start(f32[96,768]{1,0:T(8,128)} %param.13) | copy-start | bytes 884740
  222.4 2.4 %copy-start.7 = (f32[2,96,768]{2,1,0:T(8,128)S(1)}, f32[2,96,768]{2,1,0:T(8,128)}, u32[]{:S(2)}) copy-start(f32[2,96,768]{2,1,0:T(8,128)} %param.16) | copy-start | bytes 1769476
  224.9 1.0 copy-start.15
  224.9 1.0 copy-start.9
  226.5 2.8 %copy-start.3 = (f32[24,6144]{1,0:T(8,128)S(1)}, f32[24,6144]{1,0:T(8,128)}, u32[]{:S(2)}) copy-start(f32[24,6144]{1,0:T(8,128)} %get-tuple-element.103) | copy-start | bytes 1769476

commit v3 on v2

--- a/solution.py
+++ b/solution.py
@@ -279,7 +279,9 @@
             pltpu.SemaphoreType.DMA((copies,)),
             pltpu.SemaphoreType.DMA((copies,)),
         ],
-        compiler_params=pltpu.CompilerParams(collective_id=0, has_side_effects=True),
+        compiler_params=pltpu.CompilerParams(
+            collective_id=0, has_side_effects=True, vmem_limit_bytes=4 * 2**20
+        ),
     )(wide, proj, vec)
     return (
         wide_out.reshape(n * wide.shape[0], wide.shape[1]),
@@ -528,7 +530,7 @@
             pltpu.SemaphoreType.DMA((copies,)),
         ],
         compiler_params=pltpu.CompilerParams(
-            collective_id=1, has_side_effects=True, vmem_limit_bytes=52 * 2**20
+            collective_id=1, has_side_effects=True, vmem_limit_bytes=40 * 2**20
         ),
     )(
         left(first_in, "cxy"),

time: 231 us -> 240 us (1.039)
  local copies, waits for them, and re-layouts: 10.4 us -> 22.4 us
  Pallas kernels: 172 us -> 169 us
    unnamed x64 -> x78, local copies, waits for them, and re-layouts: 3.56 us -> 13.7 us
    pallas_call x1, Pallas kernels: 97.2 us -> 94.8 us  [scatter_all(): pl.pallas_call(functools.partial(scatter_kernel, n), out_shape=(jax.Shape...]
where the time goes in v3:
time: 240 us; the launch traced here: 239 us
  Pallas kernels  169 us (70%)
  matrix products  30.7 us (13%)
  local copies, waits for them, and re-layouts  22.4 us (9%)
  other arithmetic  15.5 us (6%)
    pallas_call x1, Pallas kernels, scatter_all(): pl.pallas_call(functools.partial(scatter_kernel, n), out_shape=(jax.Shape...  94.8 us
    pallas_call x1, Pallas kernels, gather_all(): pl.pallas_call(functools.partial(gather_kernel, n), out_shape=out, in_spe...  74.5 us
    unnamed x78, local copies, waits for them, and re-layouts  13.7 us
    another operation x5, other arithmetic, adam_update(): return (updated, jnp.stack([first_moment, second_moment]))  5.7 us
    dot_general x1, matrix products, body(): jnp.einsum('td,fd->tf', cotangent, backward_proj, preferred_element_type=...  5.36 us
    dot_general x1, matrix products, body(): jnp.dot(second_in, wide_full[:, 4 * D:], preferred_element_type=jnp.float32)  5.04 us

profile of v3, /device:TPU:0, one launch (start us, length us, event | category | flops | bytes accessed | tf_op | source)
XLA Modules:
  0.0 239.3 jit_solution(4062433341801039335)
XLA Ops:
  0.7 1.1 convert_element_type.80.wide
  1.8 1.0 convert_element_type.81.proj
  3.6 74.5 %shard_map.176 = (bf16[4,2,2,2,24,6144]{5,4,3,2,1,0:T(8,128)(2,1)S(1)}, bf16[4,2,2,2,96,768]{5,4,3,2,1,0:T(8,128)(2,1)S(1)}, f32[4,2,2,2,8,128]{5,4,3,2,1,0:T(8,128)S(1)}) custom-call(bf16[24,6144]{1,0:T(8,128)(2,1)S(1)} %convert_element_type.80.wide, bf16[96,768]{1,0:T(8,128)(2,1)S(1)} %convert_element_type.81.proj, f32[8,128]{1,0:T(8,128)S(1)} %bitcast.172), custom_call_target="tpu_custom_call" | custom-call | tf_op jit(solution)/shard_map/pallas_call | solution.py:272
  78.1 3.6 %copy-done.6 = bf16[4,2,2,2,24,6144]{5,4,3,2,1,0:T(8,128)(2,1)} copy-done((bf16[4,2,2,2,24,6144]{5,4,3,2,1,0:T(8,128)(2,1)}, bf16[4,2,2,2,24,6144]{5,4,3,2,1,0:T(8,128)(2,1)S(1)}, u32[]{:S(2)}) %copy-start.6) | copy-done | bytes 9437208
  81.7 2.2 copy-done.7
  86.1 2.7 %fusion.10 = bf16[128,2304]{1,0:T(8,128)(2,1)S(1)} fusion(bf16[768,6144]{1,0:T(8,128)(2,1)} %bitcast.163, f32[2304]{0:T(1024)S(1)} %pad_maximum_fusion.4, bf16[128,768]{1,0:T(8,128)(2,1)S(1)} %copy-done.8, f32[768]{0:T(1024)S(1)} %add.173, f32[768]{0:T(1024)S(1)} %mul.346, f32[128]{0:T(128)S(1)} %add_rsqrt_fusion.1, f32[128]{0:T(128)S(1)} %broadcast_multiply_fusion.5), kind=kOutput, calls=%fused_computation.10 | convolution fusion | flops 454164480 | bytes 4341760 | tf_op jit(solution)/shard_map/dot_general | solution.py:609
  90.6 1.7 fusion.101
  93.0 5.0 %fusion.23 = (bf16[3072,128]{0,1:T(8,128)(2,1)}, f32[128,3072]{1,0:T(8,128)}) fusion(f32[3072]{0:T(1024)S(1)} %add.187, bf16[768,6144]{1,0:T(8,128)(2,1)} %bitcast.165, f32[128,768]{1,0:T(8,128)S(1)} %get-tuple-element.83, f32[768]{0:T(1024)S(1)} %add.184, f32[768]{0:T(1024)S(1)} %mul.353, f32[128]{0:T(128)S(1)} %add_rsqrt_fusion, ...), kind=kOutput, calls=%fused_computation.26 | convolution fusion | flops 608403456 | bytes 7490560 | tf_op jit(solution)/shard_map/dot_general | solution.py:623
  98.2 4.7 %fusion.31 = bf16[128,768]{1,0:T(8,128)(2,1)} fusion(f32[128,768]{1,0:T(8,128)S(1)} %get-tuple-element.83, bf16[3072,768]{1,0:T(8,128)(2,1)} %bitcast.174, f32[128,3072]{1,0:T(8,128)} %get-tuple-element.85, f32[768]{0:T(1024)S(1)} %add.193), kind=kOutput, calls=%fused_computation.41 | convolution fusion | flops 607813632 | bytes 6884352 | tf_op jit(solution)/shard_map/dot_general | solution.py:628
  102.9 5.4 %convert_reduce_fusion = (f32[3072]{0:T(1024)}, bf16[128,3072]{1,0:T(8,128)(2,1)S(1)}) fusion(f32[128,3072]{1,0:T(8,128)} %get-tuple-element.85, bf16[3072,768]{1,0:T(8,128)(2,1)} %bitcast.175, bf16[128,768]{1,0:T(8,128)(2,1)S(1)} %copy-done.4), kind=kOutput, calls=%fused_computation.28 | convolution fusion | flops 612234240 | bytes 7286784 | tf_op jit(solution)/shard_map/td,fd->tf/dot_general | solution.py:637
  108.3 1.7 fusion.1
  110.0 1.5 multiply_reduce_fusion.1
  111.5 0.8 fusion.96
  114.3 1.2 fusion.102
  115.5 1.8 convolution_convert_fusion.1
  117.4 1.7 convolution_convert_fusion.2
  119.4 3.3 %fusion.11 = f32[128,768]{1,0:T(8,128)S(1)} fusion(bf16[768,6144]{1,0:T(8,128)(2,1)} %bitcast.166, bf16[128,768]{1,0:T(8,128)(2,1)S(1)} %copy.97, bf16[128,768]{1,0:T(8,128)(2,1)S(1)} %copy.96, bf16[128,768]{1,0:T(8,128)(2,1)S(1)} %copy.95), kind=kOutput, calls=%fused_computation.11 | convolution fusion | flops 454754304 | bytes 4521984 | tf_op jit(solution)/shard_map/tc,dc->td/dot_general | solution.py:662
  122.7 0.8 fusion.56
  123.5 0.9 fusion.55
  124.8 0.9 copy.102
  126.4 1.5 copy.104
  129.7 1.1 convert_reduce_fusion.4
  131.9 0.9 copy-done
  132.8 0.9 copy-done.1
  133.8 0.9 copy-done.3
  134.7 0.9 copy-done.5
  135.6 94.8 %shard_map.177 = (f32[24,6144]{1,0:T(8,128)S(1)}, f32[96,768]{1,0:T(8,128)S(1)}, f32[8,128]{1,0:T(8,128)S(1)}) custom-call(bf16[2,2,2,96,128]{4,3,2,1,0:T(8,128)(2,1)S(1)} %bitcast.158, bf16[2,2,2,96,128]{4,3,2,1,0:T(8,128)(2,1)S(1)} %bitcast.159, bf16[2,2,2,96,128]{4,3,2,1,0:T(8,128)(2,1)S(1)} %bitcast.160, bf16[2,2,2,96,128]{4,3,2,1,0:T(8,128)(2,1)S(1)} %bitcast.161, ...), custom_call_target="tpu_custom_call" | custom-call | tf_op jit(solution)/shard_map/pallas_call | solution.py:508
  230.6 2.8 %fusion.64 = (f32[1,24,6144]{2,1,0:T(8,128)S(1)}, f32[1,24,6144]{2,1,0:T(8,128)S(1)}, f32[24,6144]{1,0:T(8,128)}) fusion(f32[24,6144]{1,0:T(8,128)S(1)} %get-tuple-element.103, f32[2,24,6144]{2,1,0:T(8,128)} %param.15, f32[24,6144]{1,0:T(8,128)} %param.12), kind=kLoop, calls=%fused_computation.99 | loop fusion | flops 2359296 | bytes 4128768 | tf_op jit(solution)/shard_map/stack | solution.py:130
  233.4 1.0 fusion.68
  235.0 1.1 pad_maximum_fusion
  236.1 0.9 pad_maximum_fusion.2
  237.7 0.8 copy.170
  (155 shorter events, 13.7 us)
Async XLA Ops:
  0.6 84.3 %copy-start.8 = (bf16[128,768]{1,0:T(8,128)(2,1)S(1)}, bf16[128,768]{1,0:T(8,128)(2,1)}, u32[]{:S(2)}) copy-start(bf16[128,768]{1,0:T(8,128)(2,1)} %param.9) | copy-start | bytes 589828
  78.1 3.6 %copy-start.6 = (bf16[4,2,2,2,24,6144]{5,4,3,2,1,0:T(8,128)(2,1)}, bf16[4,2,2,2,24,6144]{5,4,3,2,1,0:T(8,128)(2,1)S(1)}, u32[]{:S(2)}) copy-start(bf16[4,2,2,2,24,6144]{5,4,3,2,1,0:T(8,128)(2,1)S(1)} %get-tuple-element.18) | copy-start | bytes 28311556
  81.7 2.2 copy-start.7
  85.1 0.5 copy-start.23
  85.6 0.5 copy-start.25
  88.8 0.7 copy-start.27
  98.2 4.7 %copy-start.4 = (bf16[128,768]{1,0:T(8,128)(2,1)S(1)}, bf16[128,768]{1,0:T(8,128)(2,1)}, u32[]{:S(2)}) copy-start(bf16[128,768]{1,0:T(8,128)(2,1)} %cot.1) | copy-start | bytes 589828
  98.2 10.1 %slice-start = ((s8[9437184]{0:T(1024)(128)(4,1)}), s8[4194304]{0:T(1024)(128)(4,1)S(1)}, s32[]{:S(2)}) async-start(s8[9437184]{0:T(1024)(128)(4,1)} %bitcast.167), calls=%async_computation | async-start | bytes 8388608
  98.2 10.1 %slice-start.1 = ((s8[9437184]{0:T(1024)(128)(4,1)}), s8[4194304]{0:T(1024)(128)(4,1)S(1)}, s32[]{:S(2)}) async-start(s8[9437184]{0:T(1024)(128)(4,1)} %bitcast.167), calls=%async_computation.1 | async-start | bytes 8388608
  102.9 5.4 %slice-start.2 = ((s8[9437184]{0:T(1024)(128)(4,1)}), s8[1048576]{0:T(1024)(128)(4,1)S(1)}, s32[]{:S(2)}) async-start(s8[9437184]{0:T(1024)(128)(4,1)} %bitcast.167), calls=%async_computation.2 | async-start | bytes 2097152
  112.9 0.7 copy-start.2
  114.3 5.0 %copy-start.10 = (bf16[128,768]{1,0:T(8,128)(2,1)}, bf16[128,768]{1,0:T(8,128)(2,1)S(1)}, u32[]{:S(2)}) copy-start(bf16[128,768]{1,0:T(8,128)(2,1)S(1)} %copy.97) | copy-start | bytes 589828
  119.2 3.5 %copy-start.12 = (bf16[12,64,128]{2,1,0:T(8,128)(2,1)}, bf16[12,64,128]{2,1,0:T(8,128)(2,1)S(1)}, u32[]{:S(2)}) copy-start(bf16[12,64,128]{2,1,0:T(8,128)(2,1)S(1)} %convolution_convert_fusion.2) | copy-start | bytes 589828
  119.3 3.3 %copy-start.24 = (f32[128]{0:T(128)S(1)}, f32[128]{0:T(128)}, u32[]{:S(2)}) copy-start(f32[128]{0:T(128)} %copy-done.23) | copy-start | bytes 1540
  119.4 3.3 %copy-start.26 = (f32[128]{0:T(128)S(1)}, f32[128]{0:T(128)}, u32[]{:S(2)}) copy-start(f32[128]{0:T(128)} %copy-done.25) | copy-start | bytes 1540
  122.7 1.9 copy-start.13
  126.4 1.7 copy-start.11
  127.9 3.2 %copy-start.20 = (f32[768]{0:T(1024)S(1)}, f32[768]{0:T(1024)}, u32[]{:S(2)}) copy-start(f32[768]{0:T(1024)} %get-tuple-element.56) | copy-start | bytes 9220
  127.9 3.3 %copy-start.18 = (f32[768]{0:T(1024)S(1)}, f32[768]{0:T(1024)}, u32[]{:S(2)}) copy-start(f32[768]{0:T(1024)} %get-tuple-element.45) | copy-start | bytes 9220
  127.9 3.4 %copy-start.17 = (f32[768]{0:T(1024)S(1)}, f32[768]{0:T(1024)}, u32[]{:S(2)}) copy-start(f32[768]{0:T(1024)} %get-tuple-element.51) | copy-start | bytes 9220
  127.9 3.5 %copy-start.19 = (f32[768]{0:T(1024)S(1)}, f32[768]{0:T(1024)}, u32[]{:S(2)}) copy-start(f32[768]{0:T(1024)} %get-tuple-element.69) | copy-start | bytes 9220
  128.0 3.5 %copy-start.21 = (f32[3072]{0:T(1024)S(1)}, f32[3072]{0:T(1024)}, u32[]{:S(2)}) copy-start(f32[3072]{0:T(1024)} %get-tuple-element.86) | copy-start | bytes 36868
  131.9 0.9 copy-start
  132.8 0.9 copy-start.1
  133.8 0.9 copy-start.3
  134.7 0.9 copy-start.5
  230.5 3.8 %copy-start.15 = (f32[12,24]{1,0:T(8,128)}, f32[12,24]{1,0:T(8,128)S(1)}, u32[]{:S(2)}) copy-start(f32[12,24]{1,0:T(8,128)S(1)} %squeeze_reshape.10) | copy-start | bytes 3460
  230.5 2.8 %copy-start.9 = (f32[96,768]{1,0:T(8,128)S(1)}, f32[96,768]{1,0:T(8,128)}, u32[]{:S(2)}) copy-start(f32[96,768]{1,0:T(8,128)} %param.13) | copy-start | bytes 884740
  230.5 2.8 %copy-start.14 = (f32[2,96,768]{2,1,0:T(8,128)S(1)}, f32[2,96,768]{2,1,0:T(8,128)}, u32[]{:S(2)}) copy-start(f32[2,96,768]{2,1,0:T(8,128)} %param.16) | copy-start | bytes 1769476
  233.3 1.0 copy-start.22
  233.3 1.0 copy-start.16

commit v4 on v2

--- a/solution.py
+++ b/solution.py
@@ -466,14 +466,15 @@
     ]
     stage_last(1)
     stage_third(2)
+    finish(0)
     stage_last(2)
     total = vec_kept[x, y, z]
     for d in range(depth - 1):
         vec_last[d].wait_recv()
         total += vec_z[d]
     vec_out[...] = total
-    for k in range(3):
-        finish(k)
+    finish(1)
+    finish(2)
     for k in range(3):
         for s in range(2):
             for t in range(4):
@@ -556,6 +557,62 @@
     return tiles.reshape(tiles.shape[0], 1024)[:, : rows * columns].reshape(-1, rows, columns)
 
 
+MLP_TILE = 512
+
+
+def mlp_kernel(second_in, cot, wide, proj, bias, hidden_out, pre_out, mixed, second_grad, bias_out):
+    @pl.when(pl.program_id(0) == 0)
+    def _():
+        mixed[...] = jnp.zeros_like(mixed)
+        second_grad[...] = jnp.zeros_like(second_grad)
+
+    before = (
+        jnp.dot(second_in[...], wide[...], preferred_element_type=jnp.float32) + bias[...]
+    )
+    value_part, slope_part = gelu_parts(before)
+    hidden = value_part.astype(jnp.bfloat16)
+    hidden_out[...] = hidden
+    mixed[...] += jnp.dot(hidden, proj[...], preferred_element_type=jnp.float32)
+    across = (((1,), (1,)), ((), ()))
+    hidden_grad = lax.dot_general(
+        cot[...], proj[...], across, preferred_element_type=jnp.float32
+    )
+    pre_grad = (hidden_grad * slope_part).astype(jnp.bfloat16)
+    pre_out[...] = pre_grad
+    bias_out[...] = jnp.sum(pre_grad.astype(jnp.float32), axis=0, keepdims=True)
+    second_grad[...] += lax.dot_general(
+        pre_grad, wide[...], across, preferred_element_type=jnp.float32
+    )
+
+
+def mlp_both(second_in, cot, wide_full, proj_full, fc_bias):
+    rows = second_in.shape[0]
+    skip = 4 * D // MLP_TILE
+    whole = pl.BlockSpec((rows, D), lambda k: (0, 0))
+    tile = pl.BlockSpec((rows, MLP_TILE), lambda k: (0, k))
+    line = pl.BlockSpec((1, MLP_TILE), lambda k: (0, k))
+    return pl.pallas_call(
+        mlp_kernel,
+        grid=(FF // MLP_TILE,),
+        in_specs=[
+            whole,
+            whole,
+            pl.BlockSpec((D, MLP_TILE), lambda k: (0, k + skip)),
+            pl.BlockSpec((MLP_TILE, D), lambda k: (k, 0)),
+            line,
+        ],
+        out_specs=(tile, tile, whole, whole, line),
+        out_shape=(
+            jax.ShapeDtypeStruct((rows, FF), jnp.bfloat16),
+            jax.ShapeDtypeStruct((rows, FF), jnp.bfloat16),
+            jax.ShapeDtypeStruct((rows, D), jnp.float32),
+            jax.ShapeDtypeStruct((rows, D), jnp.float32),
+            jax.ShapeDtypeStruct((1, FF), jnp.float32),
+        ),
+        compiler_params=pltpu.CompilerParams(vmem_limit_bytes=32 * 2**20),
+    )(second_in, cot, wide_full, proj_full, fc_bias.reshape(1, FF))
+
+
 def body(
     tokens,
     seq_lengths,
@@ -617,27 +674,16 @@
     )
     second_norm, normed_two, inverse_two = norm_forward(residual, gain_two, shift_two)
     second_in = second_norm.astype(jnp.bfloat16)
-    before_act = (
-        jnp.dot(second_in, wide_full[:, 4 * D :], preferred_element_type=jnp.float32) + fc_bias
-    )
-    value_part, slope_part = gelu_parts(before_act)
-    hidden = value_part.astype(jnp.bfloat16)
-    block_output = (
-        residual + jnp.dot(hidden, proj_full, preferred_element_type=jnp.float32) + proj_bias
-    ).astype(jnp.bfloat16)
+    hidden, pre_grad, mixed, second_grad, fc_bias_sum = mlp_both(
+        second_in, cotangent, wide_full, proj_full, fc_bias
+    )
+    block_output = (residual + mixed + proj_bias).astype(jnp.bfloat16)
     backward_wide, backward_proj, vector_again = wide_full, proj_full, vector_full
     backward_vectors = vector_again.astype(jnp.float32)
     qkv_back = backward_wide[:, : 3 * D]
     out_back = backward_wide[:, 3 * D : 4 * D]
-    fc_back = backward_wide[:, 4 * D :]
     cot_float = cotangent.astype(jnp.float32)
     proj_bias_grad = jnp.sum(cot_float, axis=0)
-    hidden_grad = jnp.einsum(
-        "td,fd->tf", cotangent, backward_proj, preferred_element_type=jnp.float32
-    )
-    pre_grad = (hidden_grad * slope_part).astype(jnp.bfloat16)
-    fc_bias_grad = jnp.sum(pre_grad, axis=0, dtype=jnp.float32)
-    second_grad = jnp.einsum("tf,df->td", pre_grad, fc_back, preferred_element_type=jnp.float32)
     resid_norm_grad, gain_two_grad, shift_two_grad = norm_backward(
         second_grad, normed_two, inverse_two, backward_vectors[5]
     )
@@ -645,7 +691,7 @@
     mlp_vectors = jnp.concatenate(
         [
             jnp.stack([gain_two_grad, shift_two_grad, proj_bias_grad]),
-            fc_bias_grad.reshape(ratio, D),
+            fc_bias_sum.reshape(ratio, D),
         ],
         axis=0,
     )

time: 231 us -> 247 us (1.069)
  local copies, waits for them, and re-layouts: 10.4 us -> 32.3 us
  matrix products: 30.7 us -> 16.2 us
  Pallas kernels: 172 us -> 179 us
    dot_general x4 -> x0, matrix products: 16.8 us -> none  [the longest x1 5.36 us: body(): jnp.einsum('td,fd->tf', cotangent, backward_proj, preferred_element_type=...]
    unnamed x64 -> x108, local copies, waits for them, and re-layouts: 3.56 us -> 18.6 us
    pallas_call x0 -> x1, Pallas kernels: none -> 6.98 us  [mlp_both(): pl.pallas_call(mlp_kernel, grid=(FF // MLP_TILE,), in_specs=[whole, whole...]
    concatenate x10, local copies, waits for them, and re-layouts: 0.74 us -> 7.37 us  [body(): vector_terms = jnp.concatenate([attn_vectors, mlp_vectors], axis=0)]
where the time goes in v4:
time: 247 us; the launch traced here: 246 us
  Pallas kernels  179 us (72%)
  local copies, waits for them, and re-layouts  32.3 us (13%)
  other arithmetic  16.7 us (7%)
  matrix products  16.2 us (7%)
    pallas_call x1, Pallas kernels, scatter_all(): pl.pallas_call(functools.partial(scatter_kernel, n), out_shape=(jax.Shape...  97.2 us
    pallas_call x1, Pallas kernels, gather_all(): pl.pallas_call(functools.partial(gather_kernel, n), out_shape=out, in_spe...  75.2 us
    unnamed x108, local copies, waits for them, and re-layouts  18.6 us
    concatenate x10, local copies, waits for them, and re-layouts, body(): vector_terms = jnp.concatenate([attn_vectors, mlp_vectors], axis=0)  7.37 us
    pallas_call x1, Pallas kernels, mlp_both(): pl.pallas_call(mlp_kernel, grid=(FF // MLP_TILE,), in_specs=[whole, whole...  6.98 us

profile of v4, /device:TPU:0, one launch (start us, length us, event | category | flops | bytes accessed | tf_op | source)
XLA Modules:
  0.0 246.1 jit_solution(16709939403368306302)
XLA Ops:
  0.7 1.8 convert_element_type.68.wide
  2.5 1.6 convert_element_type.69.proj
  4.9 75.2 %shard_map.176 = (bf16[4,2,2,2,24,6144]{5,4,3,2,1,0:T(8,128)(2,1)}, bf16[4,2,2,2,96,768]{5,4,3,2,1,0:T(8,128)(2,1)}, f32[4,2,2,2,8,128]{5,4,3,2,1,0:T(8,128)}) custom-call(bf16[24,6144]{1,0:T(8,128)(2,1)} %convert_element_type.68.wide, bf16[96,768]{1,0:T(8,128)(2,1)} %convert_element_type.69.proj, f32[8,128]{1,0:T(8,128)} %bitcast.181), custom_call_target="tpu_custom_call" | custom-call | tf_op jit(solution)/shard_map/pallas_call | solution.py:272
  80.1 0.9 copy.157
  83.1 2.7 %fusion.1 = bf16[128,2304]{1,0:T(8,128)(2,1)S(1)} fusion(bf16[768,6144]{1,0:T(8,128)(2,1)} %bitcast.143, f32[2304]{0:T(1024)S(1)} %pad_maximum_fusion.4, bf16[128,768]{1,0:T(8,128)(2,1)S(1)} %copy-done.4, f32[768]{0:T(1024)S(1)} %add.140, f32[768]{0:T(1024)S(1)} %mul.277, f32[128]{0:T(128)S(1)} %add_rsqrt_fusion.1, f32[128]{0:T(128)S(1)} %broadcast_multiply_fusion.5), kind=kOutput, calls=%fused_computation.2 | convolution fusion | flops 454164480 | bytes 4341760 | tf_op jit(solution)/shard_map/dot_general | solution.py:664
  88.0 1.7 fusion.71
  90.7 3.7 %copy-done = bf16[4,2,2,2,24,6144]{5,4,3,2,1,0:T(8,128)(2,1)S(1)} copy-done((bf16[4,2,2,2,24,6144]{5,4,3,2,1,0:T(8,128)(2,1)S(1)}, bf16[4,2,2,2,24,6144]{5,4,3,2,1,0:T(8,128)(2,1)}, u32[]{:S(2)}) %copy-start) | copy-done | bytes 9437208
  94.3 2.3 copy-done.1
  96.7 7.0 %shard_map.177 = (bf16[128,3072]{1,0:T(8,128)(2,1)S(1)}, bf16[128,3072]{1,0:T(8,128)(2,1)S(1)}, f32[128,768]{1,0:T(8,128)S(1)}, f32[128,768]{1,0:T(8,128)S(1)}, f32[1,3072]{1,0:T(1,128)S(1)}) custom-call(bf16[128,768]{1,0:T(8,128)(2,1)S(1)} %add_convert_fusion.1.second_in, bf16[128,768]{1,0:T(8,128)(2,1)S(1)} %copy-done.2, bf16[768,6144]{1,0:T(8,128)(2,1)S(1)} %bitcast.147, ...), custom_call_target="tpu_custom_call" | custom-call | tf_op jit(solution)/shard_map/pallas_call | solution.py:594
  103.7 0.9 copy-done.3
  105.5 1.5 fusion.66
  107.8 1.8 convolution_convert_fusion.3
  109.8 1.2 fusion.72
  111.0 1.9 convolution_convert_fusion.2
  113.1 1.8 convolution_convert_fusion.1
  115.1 1.1 convolution_convert_fusion
  116.4 3.3 %fusion.2 = f32[128,768]{1,0:T(8,128)S(1)} fusion(bf16[768,6144]{1,0:T(8,128)(2,1)} %bitcast.146, bf16[128,768]{1,0:T(8,128)(2,1)S(1)} %copy.96, bf16[128,768]{1,0:T(8,128)(2,1)S(1)} %copy.95, bf16[128,768]{1,0:T(8,128)(2,1)S(1)} %copy.94), kind=kOutput, calls=%fused_computation.3 | convolution fusion | flops 454754304 | bytes 4521984 | tf_op jit(solution)/shard_map/tc,dc->td/dot_general | solution.py:706
  119.8 0.9 fusion.31
  120.7 1.4 concatenate.31
  122.1 1.3 constant_dynamic-update-slice_fusion.8
  123.4 1.4 concatenate.32
  124.8 1.3 constant_dynamic-update-slice_fusion.7
  136.5 1.0 copy.106
  137.8 0.9 pad_maximum_fusion.1.qkv_g
  139.6 1.0 copy.105
  140.6 97.2 %shard_map.178 = (f32[24,6144]{1,0:T(8,128)}, f32[96,768]{1,0:T(8,128)S(1)}, f32[8,128]{1,0:T(8,128)S(1)}) custom-call(bf16[2,2,2,96,128]{4,3,2,1,0:T(8,128)(2,1)S(1)} %bitcast.152, bf16[2,2,2,96,128]{4,3,2,1,0:T(8,128)(2,1)S(1)} %bitcast.153, bf16[2,2,2,96,128]{4,3,2,1,0:T(8,128)(2,1)S(1)} %bitcast.150, bf16[2,2,2,96,128]{4,3,2,1,0:T(8,128)(2,1)S(1)} %bitcast.151, ...), custom_call_target="tpu_custom_call" | custom-call | tf_op jit(solution)/shard_map/pallas_call | solution.py:507
  238.7 1.0 fusion.43
  239.6 0.9 pad_maximum_fusion.2
  240.5 1.3 fusion.39
  241.8 1.1 pad_maximum_fusion
  243.7 0.9 fusion.30
  244.6 0.8 copy.169
  (185 shorter events, 21.7 us)
Async XLA Ops:
  0.6 3.5 %copy-start.28 = (f32[12,24]{1,0:T(8,128)S(1)}, f32[12,24]{1,0:T(8,128)}, u32[]{:S(2)}) copy-start(f32[12,24]{1,0:T(8,128)} %param.14) | copy-start | bytes 3460
  0.7 81.2 %copy-start.4 = (bf16[128,768]{1,0:T(8,128)(2,1)S(1)}, bf16[128,768]{1,0:T(8,128)(2,1)}, u32[]{:S(2)}) copy-start(bf16[128,768]{1,0:T(8,128)(2,1)} %param.9) | copy-start | bytes 589828
  87.5 2.2 copy-start.10
  89.7 15.8 %copy-start.32 = (f32[128]{0:T(128)}, f32[128]{0:T(128)S(1)}, u32[]{:S(2)}) copy-start(f32[128]{0:T(128)S(1)} %broadcast_multiply_fusion.4) | copy-start | bytes 1540
  90.0 15.6 %copy-start.35 = (f32[128]{0:T(128)}, f32[128]{0:T(128)S(1)}, u32[]{:S(2)}) copy-start(f32[128]{0:T(128)S(1)} %add_rsqrt_fusion) | copy-start | bytes 1540
  90.3 13.4 %copy-start.25 = (f32[768]{0:T(1024)}, f32[768]{0:T(1024)S(1)}, u32[]{:S(2)}) copy-start(f32[768]{0:T(1024)S(1)} %add.151) | copy-start | bytes 9220
  90.7 3.7 %copy-start = (bf16[4,2,2,2,24,6144]{5,4,3,2,1,0:T(8,128)(2,1)S(1)}, bf16[4,2,2,2,24,6144]{5,4,3,2,1,0:T(8,128)(2,1)}, u32[]{:S(2)}) copy-start(bf16[4,2,2,2,24,6144]{5,4,3,2,1,0:T(8,128)(2,1)} %get-tuple-element.23) | copy-start | bytes 28311556
  94.3 2.3 copy-start.1
  107.8 2.0 copy-start.11
  111.0 2.1 copy-start.17
  116.4 3.4 %copy-start.5 = (bf16[128,768]{1,0:T(8,128)(2,1)S(1)}, bf16[128,768]{1,0:T(8,128)(2,1)}, u32[]{:S(2)}) copy-start(bf16[128,768]{1,0:T(8,128)(2,1)} %param.9) | copy-start | bytes 589828
  116.4 3.4 %copy-start.23 = (f32[768]{0:T(1024)S(1)}, f32[768]{0:T(1024)}, u32[]{:S(2)}) copy-start(f32[768]{0:T(1024)} %copy-done.22) | copy-start | bytes 9220
  116.4 3.4 %copy-start.31 = (f32[768]{0:T(1024)S(1)}, f32[768]{0:T(1024)}, u32[]{:S(2)}) copy-start(f32[768]{0:T(1024)} %copy-done.30) | copy-start | bytes 9220
  116.4 3.4 %copy-start.38 = (f32[128]{0:T(128)S(1)}, f32[128]{0:T(128)}, u32[]{:S(2)}) copy-start(f32[128]{0:T(128)} %copy-done.37) | copy-start | bytes 1540
  116.4 3.4 %copy-start.41 = (f32[128]{0:T(128)S(1)}, f32[128]{0:T(128)}, u32[]{:S(2)}) copy-start(f32[128]{0:T(128)} %copy-done.40) | copy-start | bytes 1540
  119.8 17.9 %copy-start.12 = (f32[128,768]{1,0:T(8,128)}, f32[128,768]{1,0:T(8,128)S(1)}, u32[]{:S(2)}) copy-start(f32[128,768]{1,0:T(8,128)S(1)} %fusion.2) | copy-start | bytes 1179652
  136.5 2.1 copy-start.26
  136.5 2.1 copy-start.33
  136.5 2.1 copy-start.36
  140.6 97.3 %copy-start.34 = (f32[2,12,24]{2,0,1:T(2,128)S(1)}, f32[2,12,24]{2,0,1:T(2,128)}, u32[]{:S(2)}) copy-start(f32[2,12,24]{2,0,1:T(2,128)} %param.17) | copy-start | bytes 6916
  140.6 98.1 %copy-start.14 = (f32[96,768]{1,0:T(8,128)S(1)}, f32[96,768]{1,0:T(8,128)}, u32[]{:S(2)}) copy-start(f32[96,768]{1,0:T(8,128)} %param.13) | copy-start | bytes 884740
  140.6 98.1 %copy-start.20 = (f32[2,96,768]{2,1,0:T(8,128)S(1)}, f32[2,96,768]{2,1,0:T(8,128)}, u32[]{:S(2)}) copy-start(f32[2,96,768]{2,1,0:T(8,128)} %param.16) | copy-start | bytes 1769476
  238.7 1.8 copy-start.8
  238.7 1.8 copy-start.9
  241.8 1.9 copy-start.44
  241.8 1.9 copy-start.43
  241.8 1.9 copy-start.7
  241.8 1.9 copy-start.13
  241.8 1.9 copy-start.24
  241.8 1.9 copy-start.39
  241.8 1.9 copy-start.42
  243.0 2.4 copy-start.27
  (14 other events, 13.1 us)
